TPU v7x, 256 devices: a whole 4x4x8 slice. The times are simulated.
256 devices in a mesh: ctx: 32 (over x, y, core), head: 8 (over z).
Axes of the slice: x: 4, y: 4, z: 8, core: 2. Of those that a mesh axis runs over, the one named last changes fastest.
Arguments:
- query_proj: bfloat16 [16384, 2048], P('ctx', 'head'), may hold values from -32 to 32
- projected_keys: bfloat16 [16384, 1024], P('ctx', 'head'), may hold values from -32 to 32
- projected_values: bfloat16 [16384, 1024], P('ctx', 'head'), may hold values from -12 to 12
- w_out: bfloat16 [2048, 4096], P('head'), may hold values from -0.1875 to 0.1875
- attended_blocks: int32 [32, 12], replicated, may hold values from -1 to 31, as said below
- grad_out: bfloat16 [16384, 4096], P('ctx', 'head'), may hold values from -6 to 6
Outputs:
- layer_out: bfloat16 [16384, 4096], P('ctx', 'head')
- grad_query: float32 [16384, 2048], P('ctx', 'head')
- grad_key: float32 [16384, 1024], P('ctx', 'head')
- grad_value: float32 [16384, 1024], P('ctx', 'head')
- grad_wout: float32 [2048, 4096], P('head', 'ctx')
Inputs may be any that keep to these rules, and one draw needn't show every extreme that they name: `attended_blocks`: row b lists key blocks: its first entry is b; if b >= 16 its second entry is b - 16; the other live entries are distinct blocks among b - 11 to b - 1; -1 fills the unused entries. Row b has between min(2, b + 1) and 12 live entries, and some row has exactly 12.
All inputs are finite; a program needn't handle non-finite values.
Results may differ from a plain program's by a relative error of at most 0.04.
Values may be sent and summed in bfloat16 or wider, within the bound.
No kernel may reach another device: no remote copies, remote signals or barrier semaphores. Data moves between devices by JAX's collectives and lax.ppermute only.
A program may use at most 128 MiB of HBM per device.

v0:
```python
import functools

import jax
import jax.numpy as jnp
from jax import lax
from jax.experimental import pallas as pl
from jax.experimental.pallas import tpu as pltpu
from jax.sharding import PartitionSpec as P

HEAD_SIZE = 128
BT = 512
KV = 2 * BT
NB = 32
SCALE = HEAD_SIZE**-0.5
LOG2E = 1.4426950408889634
C2 = SCALE * LOG2E
ROWS = 256
F32 = jnp.float32
BF16 = jnp.bfloat16


VM = pl.BlockSpec(memory_space=pltpu.VMEM)
SM = pl.BlockSpec(memory_space=pltpu.SMEM)
ANY = pl.BlockSpec(memory_space=pl.ANY)


def dot_t(a, b):
    return lax.dot_general(a, b, (((1,), (1,)), ((), ())), preferred_element_type=F32)


def fetch(flags, base, sources, buf, sems):
    for e, (ref, row) in enumerate(sources):
        @pl.when(flags[2 * (base + e)] + flags[2 * (base + e) + 1] > 0)
        def _():
            pltpu.make_async_copy(ref.at[pl.ds(row, KV)], buf.at[e], sems.at[e]).start()


def walk(visit, n, diag):
    if diag:
        lax.fori_loop(0, 2, lambda i, carry: visit(True, i * diag, carry), 0)
        lax.fori_loop(0, n - 2, lambda i, carry: visit(False, jnp.where(i < diag - 1, i + 1, i + 2), carry), 0)
    else:
        lax.fori_loop(0, n, lambda i, carry: visit(False, i, carry), 0)


def fwd_body(base, plan, diag, first, last, *refs):
    n = len(plan)
    count = 1 + max(i for i, _ in plan)
    flags, q_ref = refs[0], refs[1]
    pos = 2
    if not first:
        m_in, l_in, acc_in = refs[pos : pos + 3]
        pos += 3
    arrays = refs[pos : pos + count]
    pos += count
    if last:
        own_ref, sib_ref, lse_ref = refs[pos : pos + 3]
        pos += 3
    m_ref, l_ref, acc_ref = refs[pos : pos + 3]
    buf, sems = refs[pos + 3 : pos + 5]
    fetch(flags, base, [(arrays[i], row) for i, row in plan], buf, sems)
    if first:
        m_ref[...] = jnp.full(m_ref.shape, -jnp.inf, F32)
        l_ref[...] = jnp.zeros(l_ref.shape, F32)
        acc_ref[...] = jnp.zeros(acc_ref.shape, F32)
    else:
        m_ref[...] = m_in[...]
        l_ref[...] = l_in[...]
        acc_ref[...] = acc_in[...]

    def unit(e, h, masked):
        k = buf[e, :BT, :]
        v = buf[e, BT:, :]
        for r in range(0, BT, ROWS):
            s = dot_t(q_ref[h, r : r + ROWS, :], k) * C2
            if masked:
                row = lax.broadcasted_iota(jnp.int32, (ROWS, BT), 0) + r
                col = lax.broadcasted_iota(jnp.int32, (ROWS, BT), 1)
                near = jnp.where((e == 0) & (h == 0) | (e == diag) & (h == 1), 0, BT)
                s = jnp.where(col <= row + near, s, -jnp.inf)
            at = slice(r, r + ROWS)
            m_old = m_ref[h, at, :]
            m_new = jnp.maximum(m_old, jnp.max(s, axis=1, keepdims=True))
            alpha = jnp.exp2(m_old - m_new)
            p = jnp.exp2(s - m_new[:, :1])
            m_ref[h, at, :] = m_new
            l_ref[h, at, :] = l_ref[h, at, :] * alpha + jnp.sum(p, axis=1, keepdims=True)
            acc_ref[h, at, :] = acc_ref[h, at, :] * alpha + jnp.dot(
                p.astype(BF16), v, preferred_element_type=F32
            )

    def visit(masked, e, carry):
        @pl.when(flags[2 * (base + e)] + flags[2 * (base + e) + 1] > 0)
        def _():
            pltpu.make_async_copy(arrays[0].at[pl.ds(0, KV)], buf.at[e], sems.at[e]).wait()

            def one(h, c2):
                @pl.when(flags[2 * (base + e) + h] > 0)
                def _():
                    unit(e, h, masked)

                return c2

            lax.fori_loop(0, 2, one, 0)

        return carry

    walk(visit, n, diag)
    if last:
        for h, ref in ((0, own_ref), (1, sib_ref)):
            total = l_ref[h]
            ref[...] = (acc_ref[h] / total).astype(BF16)
            lse_ref[h : h + 1, :] = jnp.transpose(m_ref[h] + jnp.log2(total))[0:1, :]


def fwd_call(flags, base, q2, state, arrays, plan, diag=0, last=False):
    n = len(plan)
    first = state is None
    state_shape = (2, BT, HEAD_SIZE)
    scratch = [pltpu.VMEM((n, KV, HEAD_SIZE), BF16), pltpu.SemaphoreType.DMA((n,))]
    if last:
        out_shape = (
            jax.ShapeDtypeStruct((BT, HEAD_SIZE), BF16),
            jax.ShapeDtypeStruct((BT, HEAD_SIZE), BF16),
            jax.ShapeDtypeStruct((2, BT), F32),
        )
        scratch = [pltpu.VMEM(state_shape, F32)] * 3 + scratch
    else:
        out_shape = (jax.ShapeDtypeStruct(state_shape, F32),) * 3
    return pl.pallas_call(
        functools.partial(fwd_body, base, plan, diag, first, last),
        out_shape=out_shape,
        in_specs=[SM, VM] + ([] if first else [VM] * 3) + [ANY] * len(arrays),
        out_specs=tuple(VM for _ in out_shape),
        scratch_shapes=scratch,
        name="fwd",
        cost_estimate=pl.CostEstimate(flops=n * 268435456, transcendentals=n * 524288, bytes_accessed=n * 262144),
    )(flags, q2, *(() if first else state), *arrays)


def bwd_body(base, plan, diag, first, last, *refs):
    n = len(plan)
    half = n // 2
    count = 1 + max(i for i, _ in plan)
    flags, q_ref, do_ref, own_ref, sib_ref, lse_ref = refs[:6]
    pos = 6
    if not first:
        dq_in = refs[pos]
        pos += 1
    arrays = refs[pos : pos + count]
    pos += count
    if last:
        dq_own, dq_sib = refs[pos : pos + 2]
        pos += 2
    else:
        dq_out = refs[pos]
        pos += 1
    keep_ref, give_ref = refs[pos : pos + 2]
    pos += 2
    dq, delta_ref, dkv, buf, obuf, sems, osems = refs[pos : pos + 7]
    fetch(flags, base, [(arrays[i], row) for i, row in plan], buf, sems)
    dq[...] = jnp.zeros(dq.shape, F32) if first else dq_in[...]
    for h, ref in ((0, own_ref), (1, sib_ref)):
        prod = do_ref[h].astype(F32) * ref[...].astype(F32)
        delta_ref[h : h + 1, :] = jnp.sum(jnp.transpose(prod), axis=0, keepdims=True)

    def unit(e, h, masked):
        q = q_ref[h]
        do = do_ref[h]
        lse = lse_ref[pl.ds(h, 1), :]
        delta = delta_ref[pl.ds(h, 1), :]
        for r in range(0, BT, ROWS):
            at = slice(r, r + ROWS)
            vt = slice(BT + r, BT + r + ROWS)
            k = buf[e, at, :]
            p = jnp.exp2(dot_t(k, q) * C2 - lse)
            if masked:
                row = lax.broadcasted_iota(jnp.int32, (ROWS, BT), 0) + r
                col = lax.broadcasted_iota(jnp.int32, (ROWS, BT), 1)
                near = jnp.where((e == 0) & (h == 0) | (e == diag) & (h == 1), 0, BT)
                p = jnp.where(row <= col + near, p, 0.0)
            ds = (p * (dot_t(buf[e, vt, :], do) - delta) * SCALE).astype(BF16)
            dkv[vt, :] += jnp.dot(p.astype(BF16), do, preferred_element_type=F32)
            dkv[at, :] += jnp.dot(ds, q, preferred_element_type=F32)
            dq[h] += lax.dot_general(k, ds, (((0,), (0,)), ((), ())), preferred_element_type=F32)

    def visit(masked, e, carry):
        on = flags[2 * (base + e)] + flags[2 * (base + e) + 1] > 0

        @pl.when(on)
        def _():
            pltpu.make_async_copy(arrays[0].at[pl.ds(0, KV)], buf.at[e], sems.at[e]).wait()
            dkv[...] = jnp.zeros(dkv.shape, F32)

            def one(h, c2):
                @pl.when(flags[2 * (base + e) + h] > 0)
                def _():
                    unit(e, h, masked)

                return c2

            lax.fori_loop(0, 2, one, 0)
            obuf[e] = dkv[...].astype(BF16)

        @pl.when(jnp.logical_not(on))
        def _():
            obuf[e] = jnp.zeros((KV, HEAD_SIZE), BF16)

        @pl.when(e < half)
        def _():
            pltpu.make_async_copy(obuf.at[e], keep_ref.at[pl.ds(e * KV, KV)], osems.at[e]).start()

        @pl.when(e >= half)
        def _():
            pltpu.make_async_copy(obuf.at[e], give_ref.at[pl.ds((e - half) * KV, KV)], osems.at[e]).start()

        return carry

    walk(visit, n, diag)
    if last:
        dq_own[...] = jnp.transpose(dq[0])
        dq_sib[...] = jnp.transpose(dq[1])
    else:
        dq_out[...] = dq[...]
    for e in range(n):
        pltpu.make_async_copy(obuf.at[e], keep_ref.at[pl.ds(0, KV)], osems.at[e]).wait()


def bwd_call(flags, base, q2, do2, own, sib, lse, dq, arrays, plan, diag=0, last=False):
    n = len(plan)
    first = dq is None
    dq_shape = (2, HEAD_SIZE, BT)
    head = jax.ShapeDtypeStruct((BT, HEAD_SIZE), F32)
    dq_outs = (head, head) if last else (jax.ShapeDtypeStruct(dq_shape, F32),)
    part = jax.ShapeDtypeStruct((n // 2 * KV, HEAD_SIZE), BF16)
    return pl.pallas_call(
        functools.partial(bwd_body, base, plan, diag, first, last),
        out_shape=dq_outs + (part, part),
        in_specs=[SM] + [VM] * (5 if first else 6) + [ANY] * len(arrays),
        out_specs=(VM,) * len(dq_outs) + (ANY, ANY),
        scratch_shapes=[
            pltpu.VMEM(dq_shape, F32),
            pltpu.VMEM((2, BT), F32),
            pltpu.VMEM((KV, HEAD_SIZE), F32),
            pltpu.VMEM((n, KV, HEAD_SIZE), BF16),
            pltpu.VMEM((n, KV, HEAD_SIZE), BF16),
            pltpu.SemaphoreType.DMA((n,)),
            pltpu.SemaphoreType.DMA((n,)),
        ],
        name="bwd",
        cost_estimate=pl.CostEstimate(flops=n * 671088640, transcendentals=n * 524288, bytes_accessed=n * 524288),
    )(flags, q2, do2, own, sib, lse, *(() if first else (dq,)), *arrays)


def grad_attn_body(g_ref, w_ref, out_ref, acc):
    @pl.when(pl.program_id(0) == 0)
    def _():
        acc[...] = jnp.zeros(acc.shape, F32)

    acc[...] += dot_t(g_ref[...], w_ref[...])

    @pl.when(pl.program_id(0) == pl.num_programs(0) - 1)
    def _():
        out_ref[...] = acc[...].astype(BF16)


def grad_attn_call(piece, w_out):
    rows, cols = piece.shape
    wide = 1024
    return pl.pallas_call(
        grad_attn_body,
        grid=(cols // wide,),
        out_shape=jax.ShapeDtypeStruct((rows, w_out.shape[0]), BF16),
        in_specs=[
            pl.BlockSpec((rows, wide), lambda i: (0, i)),
            pl.BlockSpec((w_out.shape[0], wide), lambda i: (0, i)),
        ],
        out_specs=pl.BlockSpec((rows, w_out.shape[0]), lambda i: (0, 0)),
        scratch_shapes=[pltpu.VMEM((rows, w_out.shape[0]), F32)],
        name="grad_attn",
        cost_estimate=pl.CostEstimate(flops=1073741824, transcendentals=0, bytes_accessed=6815744),
    )(piece, w_out)


ORDER = (0, 2, 1, 3)


def order(i):
    return (i % 2) * 2 + i // 2


def wout_body(where_ref, a_ref, *refs):
    keep_ref, give_ref, at = refs[4:]

    @pl.when(pl.program_id(0) == 0)
    def _():
        at[...] = jnp.transpose(a_ref[...])

    for i in range(4):
        term = jnp.dot(at[...], refs[i][...], preferred_element_type=F32).astype(BF16)

        @pl.when(where_ref[2] == 0)
        def _():
            keep_ref[i] = term[:, :128]
            give_ref[i] = term[:, 128:]

        @pl.when(where_ref[2] == 1)
        def _():
            keep_ref[i] = term[:, 128:]
            give_ref[i] = term[:, :128]


def wout_call(where, attn, piece):
    rows, width = attn.shape

    def column(i):
        return lambda p, w: (0, 4 * (w[0] ^ ORDER[i]) + (w[1] ^ order(p)))

    out = jax.ShapeDtypeStruct((16, width, 128), BF16)
    spec = pl.BlockSpec((4, width, 128), lambda p, w: (p, 0, 0))
    return pl.pallas_call(
        wout_body,
        grid_spec=pltpu.PrefetchScalarGridSpec(
            num_scalar_prefetch=1,
            grid=(4,),
            in_specs=[pl.BlockSpec((rows, width), lambda p, w: (0, 0))]
            + [pl.BlockSpec((rows, 256), column(i)) for i in range(4)],
            out_specs=[spec, spec],
            scratch_shapes=[pltpu.VMEM((width, rows), BF16)],
        ),
        out_shape=(out, out),
        name="wout_terms",
        cost_estimate=pl.CostEstimate(flops=1073741824, transcendentals=0, bytes_accessed=6553600),
    )(where, attn, *([piece] * 4))


def send(value, rule):
    pairs = []
    for b in range(NB):
        to = rule(b // 8, b // 2 % 4, b % 2)
        if to is not None:
            x, y, c = to
            pairs.append((b, 8 * x + 2 * y + c))
    return lax.ppermute(value, "ctx", pairs)


def swap(value):
    return send(value, lambda x, y, c: (x, y, 1 - c))


def ahead(value):
    return send(value, lambda x, y, c: (x + 1, y, c) if x < 3 else None)


def back(value):
    return send(value, lambda x, y, c: (x - 1, y, c) if x > 0 else None)


def along(value, k):
    return send(value, lambda x, y, c: (x, (y + k) % 4, c))


def bf(v):
    return v.astype(BF16)


def f32(v):
    return v.astype(F32)


def per_device(query_proj, projected_keys, projected_values, w_out, attended_blocks, grad_out):
    rank = lax.axis_index("ctx")
    x, y, c = rank // 8, rank // 2 % 4, rank % 2
    sib = rank + 1 - 2 * c

    piece = lax.all_gather(grad_out, "head", axis=1, tiled=True)

    def mine_of(v):
        return jnp.where(c == 0, v[:, :HEAD_SIZE], v[:, HEAD_SIZE:])

    def other_of(v):
        return jnp.where(c == 0, v[:, HEAD_SIZE:], v[:, :HEAD_SIZE])

    def joined(own, other):
        return jnp.where(c == 0, jnp.concatenate([own, other], 1), jnp.concatenate([other, own], 1))

    own = jnp.concatenate([projected_keys, projected_values], 0)
    x1 = ahead(own)
    ownx = swap(jnp.concatenate([projected_keys, projected_values, other_of(query_proj)], 0))
    d1 = along(jnp.where(y < 3, own, x1), 1)
    d2 = along(jnp.where(y < 2, own, x1), 2)
    d3 = along(jnp.where(y < 1, own, x1), 3)
    pre = jnp.concatenate([d1, d2, x1], 0)
    far = ahead(pre)
    prex = swap(pre)
    d3x = swap(d3)
    farx = swap(far)
    q2 = jnp.stack([mine_of(query_proj), ownx[KV:]])

    edge_d, mid_d, far_d = [0, 3], [1, 2, 4], [5, 6, 8]
    groups = ([0], [3, 1, 2, 4], edge_d, mid_d, far_d)
    keys = jnp.concatenate([b - 2 * jnp.array(d) for d in groups for b in (rank, sib)])
    lists = jnp.stack(
        [lax.dynamic_index_in_dim(attended_blocks, r, 0, keepdims=False) for r in (rank, sib)]
    )
    hit = jnp.any(lists[None] == keys[:, None, None], -1) & (keys >= 0)[:, None]
    flags = hit.astype(jnp.int32).reshape(-1)
    edge = ([own, d3, ownx, d3x], ((0, 0), (1, 0), (2, 0), (3, 0)))
    three = tuple((i, j * KV) for i in (0, 1) for j in (0, 1, 2))
    mid, outer = ([pre, prex], three), ([far, farx], three)
    near = ([d3, pre, d3x, prex], tuple((i + j, row) for i in (0, 2) for j, row in ((0, 0), (1, 0), (1, KV), (1, 2 * KV))))
    state = fwd_call(flags, 0, q2, None, [own, ownx], ((0, 0), (1, 0)), diag=1)
    state = fwd_call(flags, 2, q2, state, *near)
    attn_own, attn_sib, lse = fwd_call(flags, 20, q2, state, *outer, last=True)
    attn_other = swap(attn_sib)
    attn = joined(attn_own, attn_other)

    out_terms = bf(jnp.dot(attn, w_out, preferred_element_type=F32))
    layer_out = lax.psum_scatter(out_terms, "head", scatter_dimension=1, tiled=True)
    grad_attn = grad_attn_call(piece, w_out)
    do_sib = swap(other_of(grad_attn))
    do2 = jnp.stack([mine_of(grad_attn), do_sib])
    wkeep, wgive = wout_call(jnp.stack([x, y, c]), attn, piece)
    wcame = swap(wgive)

    def summed(n, parts, sent):
        low, high = [p[:n] for p in parts], [p[n : 2 * n] for p in parts]
        if sent is not None:
            low, high = low + [sent[:n]], high + [sent[n : 2 * n]]
        return low, bf(sum(f32(p) for p in high))

    args = (q2, do2, attn_own, attn_sib, lse)
    dq, keep, give = bwd_call(flags, 20, *args, None, *outer)
    got = swap(give)
    came = back(bf(f32(keep) + f32(got)))
    parts, gave = summed(8, [wkeep], wcame)
    wcame = send(gave, lambda x, y, c: (x, y ^ 1, c))
    dq, keep_e, give_e = bwd_call(flags, 10, *args, dq, *edge, diag=2)
    got_e = swap(give_e)
    s3 = along(bf(f32(keep_e[KV:]) + f32(got_e[KV:])), -3)
    dq_own, dq_sib, keep, give = bwd_call(flags, 14, *args, dq, *mid, last=True)
    got = swap(give)
    dq_other = swap(dq_sib)
    parts, gave = summed(4, parts, wcame)
    wcame = send(gave, lambda x, y, c: (x, y ^ 2, c))
    t1, t2, t4 = [f32(keep[at]) + f32(got[at]) + f32(came[at]) for at in (slice(i, i + KV) for i in (0, KV, 2 * KV))]
    s1 = along(bf(t1), -1)
    s2 = along(bf(t2), -2)
    parts, gave = summed(2, parts, wcame)
    wcame = send(gave, lambda x, y, c: (x ^ 1, y, c))

    def kept(cond, v):
        return jnp.where(cond, f32(v), 0.0)

    t4 = t4 + kept(y == 3, s1) + kept(y >= 2, s2) + kept(y >= 1, s3)
    r4 = back(bf(t4))
    parts, gave = summed(1, parts, wcame)
    wcame = send(gave, lambda x, y, c: (x ^ 2, y, c))
    grad_wout = sum(f32(p[0]) for p in parts) + f32(wcame[0])
    grad_query = joined(dq_own, dq_other)
    total = f32(keep_e[:KV]) + f32(got_e[:KV]) + kept(y < 3, s1) + kept(y < 2, s2) + kept(y < 1, s3) + f32(r4)
    return (layer_out, grad_query, total[:BT], total[BT:], grad_wout)


def solution(mesh):
    return jax.shard_map(
        per_device,
        mesh=mesh,
        in_specs=(
            P("ctx", "head"),
            P("ctx", "head"),
            P("ctx", "head"),
            P("head", None),
            P(),
            P("ctx", "head"),
        ),
        out_specs=(
            P("ctx", "head"),
            P("ctx", "head"),
            P("ctx", "head"),
            P("ctx", "head"),
            P("head", "ctx"),
        ),
        check_vma=False,
    )
```

profile of v0, /device:TPU:1, one launch (start us, length us, event | category | flops | bytes accessed | tf_op | source)
XLA Modules:
  0.0 186.4 jit_solution(2472403107696719881)
XLA Ops:
  7.2 0.7 all-gather.2.cloned.1.call-update
  8.0 0.9 constant_dynamic-update-slice_fusion.1
  8.9 0.9 constant_dynamic-update-slice_fusion.refs_2_.refs_7_
  9.8 3.9 %collective-permute-start.1 = (bf16[1024,128]{1,0:T(8,128)(2,1)S(1)}, bf16[1024,128]{1,0:T(8,128)(2,1)S(1)}, u32[]{:S(2)}, u32[]{:S(2)}) collective-permute-start(bf16[1024,128]{1,0:T(8,128)(2,1)S(1)} %constant_dynamic-update-slice_fusion.refs_2_.refs_7_), channel_id=1, source_target_pairs={{0,64},{8,72},{16,80},{24,88},{32,96},{40,104},{48,112},{56,120},{... | collective-permute-start | bytes 786440 | tf_op jit(solution)/shard_map/ppermute | solution.py:344
  13.8 1.0 select_bitcast_fusion.1
  14.8 1.0 pad_maximum_fusion
  15.8 1.0 collective-permute-start
  16.9 1.9 %collective-permute-done.1 = bf16[1024,128]{1,0:T(8,128)(2,1)S(1)} collective-permute-done((bf16[1024,128]{1,0:T(8,128)(2,1)S(1)}, bf16[1024,128]{1,0:T(8,128)(2,1)S(1)}, u32[]{:S(2)}, u32[]{:S(2)}) %collective-permute-start.1) | collective-permute-done | bytes 262176 | tf_op jit(solution)/shard_map/ppermute | solution.py:344
  18.8 3.0 %collective-permute-start.4 = (bf16[1024,128]{1,0:T(8,128)(2,1)S(1)}, bf16[1024,128]{1,0:T(8,128)(2,1)S(1)}, u32[]{:S(2)}, u32[]{:S(2)}) collective-permute-start(bf16[1024,128]{1,0:T(8,128)(2,1)S(1)} %get-tuple-element.51), channel_id=1, source_target_pairs={{0,32},{8,40},{16,48},{24,56},{32,0},{40,8},{48,16},{56,24},{64,96... | collective-permute-start | bytes 786440 | tf_op jit(solution)/shard_map/ppermute | solution.py:344
  22.2 11.6 %collective-permute-done.3 = bf16[1024,128]{1,0:T(8,128)(2,1)S(1)} collective-permute-done((bf16[1024,128]{1,0:T(8,128)(2,1)S(1)}, bf16[1024,128]{1,0:T(8,128)(2,1)S(1)}, u32[]{:S(2)}, u32[]{:S(2)}) %collective-permute-start.3) | collective-permute-done | bytes 262176 | tf_op jit(solution)/shard_map/ppermute | solution.py:344
  34.0 5.1 %collective-permute-start.7 = (bf16[3072,128]{1,0:T(8,128)(2,1)S(1)}, bf16[3072,128]{1,0:T(8,128)(2,1)}, u32[]{:S(2)}, u32[]{:S(2)}) collective-permute-start(bf16[3072,128]{1,0:T(8,128)(2,1)S(1)} %constant_dynamic-update-slice_fusion.2.refs_6_.refs_7_), channel_id=1, source_target_pairs={{0,64},{8,72},{16,80},{24,88},{32,96},{40,104},{48,112},{56,120},{... | collective-permute-start | bytes 2359304 | tf_op jit(solution)/shard_map/ppermute | solution.py:344
  39.2 1.2 collective-permute-start.6
  41.0 13.0 %collective-permute-done.7.refs_5_.refs_6_ = bf16[3072,128]{1,0:T(8,128)(2,1)} collective-permute-done((bf16[3072,128]{1,0:T(8,128)(2,1)S(1)}, bf16[3072,128]{1,0:T(8,128)(2,1)}, u32[]{:S(2)}, u32[]{:S(2)}) %collective-permute-start.7) | collective-permute-done | bytes 786464 | tf_op jit(solution)/shard_map/ppermute | solution.py:344
  54.0 1.8 collective-permute-start.8
  56.6 0.8 pad_maximum_fusion.1.refs_1_
  57.5 6.2 %fwd.3 = (f32[2,512,128]{2,1,0:T(8,128)}, f32[2,512,128]{2,1,0:T(8,128)}, f32[2,512,128]{2,1,0:T(8,128)}) custom-call(s32[52]{0:T(128)} %reshape.100.refs_0_, bf16[2,512,128]{2,1,0:T(8,128)(2,1)} %pad_maximum_fusion.1.refs_1_, bf16[1024,128]{1,0:T(8,128)(2,1)} %copy-done.7, bf16[1536,128]{1,0:T(8,128)(2,1)} %copy-done.13), custom_call_target="tpu_custom_call" | custom-call | flops 536870912 | bytes 524288 | tf_op jit(solution)/shard_map/fwd/pallas_call | solution.py:130
  63.7 0.7 copy-done.19
  64.4 2.9 %fwd.4 = (f32[2,512,128]{2,1,0:T(8,128)}, f32[2,512,128]{2,1,0:T(8,128)}, f32[2,512,128]{2,1,0:T(8,128)}) custom-call(s32[52]{0:T(128)} %reshape.100.refs_0_, bf16[2,512,128]{2,1,0:T(8,128)(2,1)} %pad_maximum_fusion.1.refs_1_, f32[2,512,128]{2,1,0:T(8,128)} %get-tuple-element.26.refs_2_, f32[2,512,128]{2,1,0:T(8,128)} %get-tuple-element.27.refs_3_, ...), custom_call_target="tpu_custom_call" | custom-call | flops 2147483648 | bytes 2097152 | tf_op jit(solution)/shard_map/fwd/pallas_call | solution.py:130
  67.3 2.6 %fwd.5 = (bf16[512,128]{1,0:T(8,128)(2,1)}, bf16[512,128]{1,0:T(8,128)(2,1)}, f32[2,512]{1,0:T(2,128)}) custom-call(s32[52]{0:T(128)} %reshape.100.refs_0_, bf16[2,512,128]{2,1,0:T(8,128)(2,1)} %pad_maximum_fusion.1.refs_1_, f32[2,512,128]{2,1,0:T(8,128)} %get-tuple-element.29.refs_2_, f32[2,512,128]{2,1,0:T(8,128)} %get-tuple-element.30.refs_3_, ...), custom_call_target="tpu_custom_call" | custom-call | flops 1610612736 | bytes 1572864 | tf_op jit(solution)/shard_map/fwd/pallas_call | solution.py:130
  70.5 1.2 collective-permute-done.9
  71.7 1.1 maximum_select_fusion.1.a_ref
  72.8 3.3 %convolution_convert_fusion = bf16[512,4096]{1,0:T(8,128)(2,1)} fusion(bf16[512,256]{1,0:T(8,128)(2,1)S(1)} %maximum_select_fusion.1.a_ref, bf16[256,4096]{1,0:T(8,128)(2,1)S(1)} %copy-done), kind=kOutput, calls=%fused_computation | convolution fusion | flops 1075838976 | bytes 6553600 | tf_op jit(solution)/shard_map/dot_general | solution.py:418
  76.1 5.1 %grad_attn.1 = bf16[512,256]{1,0:T(8,128)(2,1)} custom-call(bf16[512,4096]{1,0:T(8,128)(2,1)} %all-gather.2.cloned.1.call-done.g_ref.refs_0_.refs_1_.refs_2_.refs_3_, bf16[256,4096]{1,0:T(8,128)(2,1)} %w_ref.1), custom_call_target="tpu_custom_call" | custom-call | flops 1073741824 | bytes 6815744 | tf_op jit(solution)/shard_map/grad_attn/pallas_call | solution.py:270
  81.2 1.0 select_bitcast_fusion
  83.2 8.1 %wout_terms.1 = (bf16[16,256,128]{2,1,0:T(8,128)(2,1)}, bf16[16,256,128]{2,1,0:T(8,128)(2,1)}) custom-call(s32[3]{0:T(128)} %pad_add_fusion.1.where_ref, bf16[512,256]{1,0:T(8,128)(2,1)} %copy-done.1, bf16[512,4096]{1,0:T(8,128)(2,1)} %all-gather.2.cloned.1.call-done.g_ref.refs_0_.refs_1_.refs_2_.refs_3_, ...), custom_call_target="tpu_custom_call" | custom-call | flops 1073741824 | bytes 6553600 | tf_op jit(solution)/shard_map/wout_terms/pallas_call | solution.py:321
  91.4 0.7 pad_maximum_fusion.2.refs_2_
  92.2 3.4 %bwd.3 = (f32[2,128,512]{2,1,0:T(8,128)}, bf16[3072,128]{1,0:T(8,128)(2,1)}, bf16[3072,128]{1,0:T(8,128)(2,1)}) custom-call(s32[52]{0:T(128)} %reshape.100.refs_0_, bf16[2,512,128]{2,1,0:T(8,128)(2,1)} %pad_maximum_fusion.1.refs_1_, bf16[2,512,128]{2,1,0:T(8,128)(2,1)} %pad_maximum_fusion.2.refs_2_, bf16[512,128]{1,0:T(8,128)(2,1)} %get-tuple-element.32.refs_3_, ...), custom_call_target="tpu_custom_call" | custom-call | flops 4026531840 | bytes 3145728 | tf_op jit(solution)/shard_map/bwd/pallas_call | solution.py:236
  96.1 7.0 %bwd.4 = (f32[2,128,512]{2,1,0:T(8,128)}, bf16[2048,128]{1,0:T(8,128)(2,1)}, bf16[2048,128]{1,0:T(8,128)(2,1)}) custom-call(s32[52]{0:T(128)} %reshape.100.refs_0_, bf16[2,512,128]{2,1,0:T(8,128)(2,1)} %pad_maximum_fusion.1.refs_1_, bf16[2,512,128]{2,1,0:T(8,128)(2,1)} %pad_maximum_fusion.2.refs_2_, bf16[512,128]{1,0:T(8,128)(2,1)} %get-tuple-element.32.refs_3_, ...), custom_call_target="tpu_custom_call" | custom-call | flops 2684354560 | bytes 2097152 | tf_op jit(solution)/shard_map/bwd/pallas_call | solution.py:236
  103.3 3.7 %bwd.5 = (f32[512,128]{1,0:T(8,128)}, f32[512,128]{1,0:T(8,128)}, bf16[3072,128]{1,0:T(8,128)(2,1)}, bf16[3072,128]{1,0:T(8,128)(2,1)}) custom-call(s32[52]{0:T(128)} %reshape.100.refs_0_, bf16[2,512,128]{2,1,0:T(8,128)(2,1)} %pad_maximum_fusion.1.refs_1_, bf16[2,512,128]{2,1,0:T(8,128)(2,1)} %pad_maximum_fusion.2.refs_2_, ...), custom_call_target="tpu_custom_call" | custom-call | flops 4026531840 | bytes 3145728 | tf_op jit(solution)/shard_map/bwd/pallas_call | solution.py:236
  107.8 7.1 %collective-permute-start.21 = (bf16[8,256,128]{2,1,0:T(8,128)(2,1)S(1)}, bf16[8,256,128]{2,1,0:T(8,128)(2,1)S(1)}, u32[]{:S(2)}, u32[]{:S(2)}) collective-permute-start(bf16[8,256,128]{2,1,0:T(8,128)(2,1)S(1)} %add_convert_fusion.1), channel_id=1, source_target_pairs={{0,16},{8,24},{16,0},{24,8},{32,48},{40,56},{48,32},{56,40},{64,80... | collective-permute-start | bytes 1572872 | tf_op jit(solution)/shard_map/ppermute | solution.py:344
  115.0 1.4 collective-permute-start.15
  116.5 10.6 %collective-permute-done.21 = bf16[8,256,128]{2,1,0:T(8,128)(2,1)S(1)} collective-permute-done((bf16[8,256,128]{2,1,0:T(8,128)(2,1)S(1)}, bf16[8,256,128]{2,1,0:T(8,128)(2,1)S(1)}, u32[]{:S(2)}, u32[]{:S(2)}) %collective-permute-start.21) | collective-permute-done | bytes 524320 | tf_op jit(solution)/shard_map/ppermute | solution.py:344
  127.2 9.5 %collective-permute-start.22 = (bf16[4,256,128]{2,1,0:T(8,128)(2,1)S(1)}, bf16[4,256,128]{2,1,0:T(8,128)(2,1)S(1)}, u32[]{:S(2)}, u32[]{:S(2)}) collective-permute-start(bf16[4,256,128]{2,1,0:T(8,128)(2,1)S(1)} %add_convert_fusion.2), channel_id=1, source_target_pairs={{0,32},{8,40},{16,48},{24,56},{32,0},{40,8},{48,16},{56,24},{64,96... | collective-permute-start | bytes 786440 | tf_op jit(solution)/shard_map/ppermute | solution.py:344
  136.7 1.7 add_convert_fusion.3
  139.0 3.8 %collective-permute-done.22 = bf16[4,256,128]{2,1,0:T(8,128)(2,1)S(1)} collective-permute-done((bf16[4,256,128]{2,1,0:T(8,128)(2,1)S(1)}, bf16[4,256,128]{2,1,0:T(8,128)(2,1)S(1)}, u32[]{:S(2)}, u32[]{:S(2)}) %collective-permute-start.22) | collective-permute-done | bytes 262176 | tf_op jit(solution)/shard_map/ppermute | solution.py:344
  142.9 6.3 %collective-permute-start.23 = (bf16[2,256,128]{2,1,0:T(8,128)(2,1)S(1)}, bf16[2,256,128]{2,1,0:T(8,128)(2,1)}, u32[]{:S(2)}, u32[]{:S(2)}) collective-permute-start(bf16[2,256,128]{2,1,0:T(8,128)(2,1)S(1)} %add_convert_fusion.6), channel_id=1, source_target_pairs={{0,64},{8,72},{16,80},{24,88},{32,96},{40,104},{48,112},{56,120},{... | collective-permute-start | bytes 393224 | tf_op jit(solution)/shard_map/ppermute | solution.py:344
  149.2 1.2 add_convert_fusion.4
  150.4 2.7 %collective-permute-start.17 = (bf16[1024,128]{1,0:T(8,128)(2,1)}, bf16[1024,128]{1,0:T(8,128)(2,1)S(1)}, u32[]{:S(2)}, u32[]{:S(2)}) collective-permute-start(bf16[1024,128]{1,0:T(8,128)(2,1)} %get-tuple-element.47), channel_id=1, source_target_pairs={{0,32},{8,40},{16,48},{24,56},{32,0},{40,8},{48,16},{56,24},{64,96... | collective-permute-start | bytes 786440 | tf_op jit(solution)/shard_map/ppermute | solution.py:344
  153.1 3.6 %collective-permute-start.11 = (f32[512,128]{1,0:T(8,128)}, f32[512,128]{1,0:T(8,128)S(1)}, u32[]{:S(2)}, u32[]{:S(2)}) collective-permute-start(f32[512,128]{1,0:T(8,128)} %get-tuple-element.38), channel_id=1, source_target_pairs={{0,8},{8,0},{16,24},{24,16},{32,40},{40,32},{48,56},{56,48},{64,72... | collective-permute-start | bytes 786440 | tf_op jit(solution)/shard_map/ppermute | solution.py:344
  156.7 0.9 add_convert_fusion.7
  157.7 6.9 %collective-permute-start.24 = (bf16[1,256,128]{2,1,0:T(8,128)(2,1)S(1)}, bf16[1,256,128]{2,1,0:T(8,128)(2,1)S(1)}, u32[]{:S(2)}, u32[]{:S(2)}) collective-permute-start(bf16[1,256,128]{2,1,0:T(8,128)(2,1)S(1)} %add_convert_fusion.7), channel_id=1, source_target_pairs={{0,128},{8,136},{16,144},{24,152},{32,160},{40,168},{48,176},{56,1... | collective-permute-start | bytes 196616 | tf_op jit(solution)/shard_map/ppermute | solution.py:344
  164.6 1.4 fusion.7
  166.0 1.3 collective-permute-start.19
  167.3 0.8 maximum_select_fusion
  168.1 1.6 add_bitcast_fusion
  169.7 7.8 %collective-permute-done.19 = bf16[1024,128]{1,0:T(8,128)(2,1)S(1)} collective-permute-done((bf16[1024,128]{1,0:T(8,128)(2,1)S(1)}, bf16[1024,128]{1,0:T(8,128)(2,1)S(1)}, u32[]{:S(2)}, u32[]{:S(2)}) %collective-permute-start.19) | collective-permute-done | bytes 262176 | tf_op jit(solution)/shard_map/ppermute | solution.py:344
  177.5 1.2 fusion.3
  178.7 0.8 fusion.10
  (95 shorter events, 6.4 us)
Async XLA Ops:
  7.2 15.0 %copy-start.16 = (s32[3]{0:T(128)S(1)}, s32[3]{0:T(128)}, u32[]{:S(2)}) copy-start(s32[3]{0:T(128)} %constant.94) | copy-start | bytes 40
  7.2 15.0 %copy-start.17 = (s32[3]{0:T(128)S(1)}, s32[3]{0:T(128)}, u32[]{:S(2)}) copy-start(s32[3]{0:T(128)} %constant.92) | copy-start | bytes 40
  7.2 68.9 %all-gather.2.cloned.1.call-start = ((), (), s32[]{:S(2)}) async-start(), calls=%async_computation.2 | async-start | bytes 4718592 | tf_op jit(solution)/shard_map/all_gather | solution.py:376
  7.9 171.6 %reduce-scatter.2.cloned.1.call-start = ((), (), s32[]{:S(2)}) async-start(), calls=%async_computation.1 | async-start | bytes 4718592 | tf_op jit(solution)/shard_map/reduce_scatter | solution.py:419
  9.8 24.1 %copy-start.7 = (bf16[1024,128]{1,0:T(8,128)(2,1)}, bf16[1024,128]{1,0:T(8,128)(2,1)S(1)}, u32[]{:S(2)}) copy-start(bf16[1024,128]{1,0:T(8,128)(2,1)S(1)} %constant_dynamic-update-slice_fusion.refs_2_.refs_7_) | copy-start | bytes 786436
  9.8 8.9 %collective-permute-start.1 = (bf16[1024,128]{1,0:T(8,128)(2,1)S(1)}, bf16[1024,128]{1,0:T(8,128)(2,1)S(1)}, u32[]{:S(2)}, u32[]{:S(2)}) collective-permute-start(bf16[1024,128]{1,0:T(8,128)(2,1)S(1)} %constant_dynamic-update-slice_fusion.refs_2_.refs_7_), channel_id=1, source_target_pairs={{0,64},{8,72},{16,80},{24,88},{32,96},{40,104},{48,112},{56,120},{... | collective-permute-start | bytes 786440 | tf_op jit(solution)/shard_map/ppermute | solution.py:344
  13.8 25.2 %copy-start.15 = (s32[4]{0:T(128)S(1)}, s32[4]{0:T(128)}, u32[]{:S(2)}) copy-start(s32[4]{0:T(128)} %constant.90) | copy-start | bytes 52
  13.8 25.3 %copy-start.14 = (s32[32,12]{0,1:T(8,128)S(1)}, s32[32,12]{0,1:T(8,128)}, u32[]{:S(2)}) copy-start(s32[32,12]{0,1:T(8,128)} %param.20) | copy-start | bytes 4612
  15.8 40.7 %collective-permute-start = (bf16[1536,128]{1,0:T(8,128)(2,1)S(1)}, bf16[1536,128]{1,0:T(8,128)(2,1)S(1)}, u32[]{:S(2)}, u32[]{:S(2)}) collective-permute-start(bf16[1536,128]{1,0:T(8,128)(2,1)S(1)} %pad_maximum_fusion), channel_id=1, source_target_pairs={{0,8},{8,0},{16,24},{24,16},{32,40},{40,32},{48,56},{56,48},{64,72... | collective-permute-start | bytes 1179656 | tf_op jit(solution)/shard_map/ppermute | solution.py:344
  18.8 15.0 %collective-permute-start.4 = (bf16[1024,128]{1,0:T(8,128)(2,1)S(1)}, bf16[1024,128]{1,0:T(8,128)(2,1)S(1)}, u32[]{:S(2)}, u32[]{:S(2)}) collective-permute-start(bf16[1024,128]{1,0:T(8,128)(2,1)S(1)} %get-tuple-element.51), channel_id=1, source_target_pairs={{0,32},{8,40},{16,48},{24,56},{32,0},{40,8},{48,16},{56,24},{64,96... | collective-permute-start | bytes 786440 | tf_op jit(solution)/shard_map/ppermute | solution.py:344
  21.8 12.0 %collective-permute-start.3 = (bf16[1024,128]{1,0:T(8,128)(2,1)S(1)}, bf16[1024,128]{1,0:T(8,128)(2,1)S(1)}, u32[]{:S(2)}, u32[]{:S(2)}) collective-permute-start(bf16[1024,128]{1,0:T(8,128)(2,1)S(1)} %get-tuple-element.52), channel_id=1, source_target_pairs={{0,16},{8,24},{16,32},{24,40},{32,48},{40,56},{48,0},{56,8},{64,80... | collective-permute-start | bytes 786440 | tf_op jit(solution)/shard_map/ppermute | solution.py:344
  33.9 29.8 %copy-start.12 = (bf16[3072,128]{1,0:T(8,128)(2,1)}, bf16[3072,128]{1,0:T(8,128)(2,1)S(1)}, u32[]{:S(2)}) copy-start(bf16[3072,128]{1,0:T(8,128)(2,1)S(1)} %constant_dynamic-update-slice_fusion.2.refs_6_.refs_7_) | copy-start | bytes 2359300
  34.0 20.1 %collective-permute-start.7 = (bf16[3072,128]{1,0:T(8,128)(2,1)S(1)}, bf16[3072,128]{1,0:T(8,128)(2,1)}, u32[]{:S(2)}, u32[]{:S(2)}) collective-permute-start(bf16[3072,128]{1,0:T(8,128)(2,1)S(1)} %constant_dynamic-update-slice_fusion.2.refs_6_.refs_7_), channel_id=1, source_target_pairs={{0,64},{8,72},{16,80},{24,88},{32,96},{40,104},{48,112},{56,120},{... | collective-permute-start | bytes 2359304 | tf_op jit(solution)/shard_map/ppermute | solution.py:344
  39.2 24.5 %collective-permute-start.6 = (bf16[3072,128]{1,0:T(8,128)(2,1)S(1)}, bf16[3072,128]{1,0:T(8,128)(2,1)}, u32[]{:S(2)}, u32[]{:S(2)}) collective-permute-start(bf16[3072,128]{1,0:T(8,128)(2,1)S(1)} %constant_dynamic-update-slice_fusion.2.refs_6_.refs_7_), channel_id=1, source_target_pairs={{0,8},{8,0},{16,24},{24,16},{32,40},{40,32},{48,56},{56,48},{64,72... | collective-permute-start | bytes 2359304 | tf_op jit(solution)/shard_map/ppermute | solution.py:344
  40.6 15.9 %collective-permute-start.2 = (bf16[1024,128]{1,0:T(8,128)(2,1)S(1)}, bf16[1024,128]{1,0:T(8,128)(2,1)S(1)}, u32[]{:S(2)}, u32[]{:S(2)}) collective-permute-start(bf16[1024,128]{1,0:T(8,128)(2,1)S(1)} %get-tuple-element.53), channel_id=1, source_target_pairs={{0,48},{8,56},{16,0},{24,8},{32,16},{40,24},{48,32},{56,40},{64,11... | collective-permute-start | bytes 786440 | tf_op jit(solution)/shard_map/ppermute | solution.py:344
  54.0 13.3 %collective-permute-start.8 = (bf16[3072,128]{1,0:T(8,128)(2,1)}, bf16[3072,128]{1,0:T(8,128)(2,1)}, u32[]{:S(2)}, u32[]{:S(2)}) collective-permute-start(bf16[3072,128]{1,0:T(8,128)(2,1)} %collective-permute-done.7.refs_5_.refs_6_), channel_id=1, source_target_pairs={{0,8},{8,0},{16,24},{24,16},{32,40},{40,32},{48,56},{56,48},{64,72... | collective-permute-start | bytes 2359304 | tf_op jit(solution)/shard_map/ppermute | solution.py:344
  56.5 7.2 %copy-start.18 = (bf16[1024,128]{1,0:T(8,128)(2,1)}, bf16[1024,128]{1,0:T(8,128)(2,1)S(1)}, u32[]{:S(2)}) copy-start(bf16[1024,128]{1,0:T(8,128)(2,1)S(1)} %collective-permute-done.2.refs_5_.refs_8_) | copy-start | bytes 786436
  56.5 7.1 %collective-permute-start.5 = (bf16[1024,128]{1,0:T(8,128)(2,1)S(1)}, bf16[1024,128]{1,0:T(8,128)(2,1)S(1)}, u32[]{:S(2)}, u32[]{:S(2)}) collective-permute-start(bf16[1024,128]{1,0:T(8,128)(2,1)S(1)} %collective-permute-done.2.refs_5_.refs_8_), channel_id=1, source_target_pairs={{0,8},{8,0},{16,24},{24,16},{32,40},{40,32},{48,56},{56,48},{64,72... | collective-permute-start | bytes 786440 | tf_op jit(solution)/shard_map/ppermute | solution.py:344
  56.6 0.9 copy-start.13
  63.7 0.7 copy-start.19
  67.3 5.5 %copy-start = (bf16[256,4096]{1,0:T(8,128)(2,1)S(1)}, bf16[256,4096]{1,0:T(8,128)(2,1)}, u32[]{:S(2)}) copy-start(bf16[256,4096]{1,0:T(8,128)(2,1)} %w_ref.1) | copy-start | bytes 6291460
  70.0 1.8 collective-permute-start.9
  72.8 3.3 %copy-start.1 = (bf16[512,256]{1,0:T(8,128)(2,1)}, bf16[512,256]{1,0:T(8,128)(2,1)S(1)}, u32[]{:S(2)}) copy-start(bf16[512,256]{1,0:T(8,128)(2,1)S(1)} %maximum_select_fusion.1.a_ref) | copy-start | bytes 786436
  82.2 9.2 %collective-permute-start.10 = (bf16[512,128]{1,0:T(8,128)(2,1)S(1)}, bf16[512,128]{1,0:T(8,128)(2,1)S(1)}, u32[]{:S(2)}, u32[]{:S(2)}) collective-permute-start(bf16[512,128]{1,0:T(8,128)(2,1)S(1)} %get-tuple-element.55), channel_id=1, source_target_pairs={{0,8},{8,0},{16,24},{24,16},{32,40},{40,32},{48,56},{56,48},{64,72... | collective-permute-start | bytes 393224 | tf_op jit(solution)/shard_map/ppermute | solution.py:344
  91.3 16.3 %collective-permute-start.20 = (bf16[16,256,128]{2,1,0:T(8,128)(2,1)}, bf16[16,256,128]{2,1,0:T(8,128)(2,1)S(1)}, u32[]{:S(2)}, u32[]{:S(2)}) collective-permute-start(bf16[16,256,128]{2,1,0:T(8,128)(2,1)} %get-tuple-element.46), channel_id=1, source_target_pairs={{0,8},{8,0},{16,24},{24,16},{32,40},{40,32},{48,56},{56,48},{64,72... | collective-permute-start | bytes 3145736 | tf_op jit(solution)/shard_map/ppermute | solution.py:344
  95.6 19.2 %collective-permute-start.14 = (bf16[3072,128]{1,0:T(8,128)(2,1)}, bf16[3072,128]{1,0:T(8,128)(2,1)S(1)}, u32[]{:S(2)}, u32[]{:S(2)}) collective-permute-start(bf16[3072,128]{1,0:T(8,128)(2,1)} %get-tuple-element.44), channel_id=1, source_target_pairs={{0,8},{8,0},{16,24},{24,16},{32,40},{40,32},{48,56},{56,48},{64,72... | collective-permute-start | bytes 2359304 | tf_op jit(solution)/shard_map/ppermute | solution.py:344
  103.1 33.6 %collective-permute-start.12 = (bf16[2048,128]{1,0:T(8,128)(2,1)}, bf16[2048,128]{1,0:T(8,128)(2,1)}, u32[]{:S(2)}, u32[]{:S(2)}) collective-permute-start(bf16[2048,128]{1,0:T(8,128)(2,1)} %get-tuple-element.40), channel_id=1, source_target_pairs={{0,8},{8,0},{16,24},{24,16},{32,40},{40,32},{48,56},{56,48},{64,72... | collective-permute-start | bytes 1572872 | tf_op jit(solution)/shard_map/ppermute | solution.py:344
  103.3 4.3 %copy-start.2 = (bf16[16,256,128]{2,1,0:T(8,128)(2,1)S(1)}, bf16[16,256,128]{2,1,0:T(8,128)(2,1)}, u32[]{:S(2)}) copy-start(bf16[16,256,128]{2,1,0:T(8,128)(2,1)} %get-tuple-element.45) | copy-start | bytes 3145732
  107.1 7.8 %copy-start.3 = (bf16[3072,128]{1,0:T(8,128)(2,1)S(1)}, bf16[3072,128]{1,0:T(8,128)(2,1)}, u32[]{:S(2)}) copy-start(bf16[3072,128]{1,0:T(8,128)(2,1)} %get-tuple-element.43) | copy-start | bytes 2359300
  107.1 42.1 %collective-permute-start.13 = (bf16[3072,128]{1,0:T(8,128)(2,1)}, bf16[3072,128]{1,0:T(8,128)(2,1)S(1)}, u32[]{:S(2)}, u32[]{:S(2)}) collective-permute-start(bf16[3072,128]{1,0:T(8,128)(2,1)} %get-tuple-element.42), channel_id=1, source_target_pairs={{0,8},{8,0},{16,24},{24,16},{32,40},{40,32},{48,56},{56,48},{64,72... | collective-permute-start | bytes 2359304 | tf_op jit(solution)/shard_map/ppermute | solution.py:344
  107.8 28.9 %copy-start.8 = (bf16[2048,128]{1,0:T(8,128)(2,1)S(1)}, bf16[2048,128]{1,0:T(8,128)(2,1)}, u32[]{:S(2)}) copy-start(bf16[2048,128]{1,0:T(8,128)(2,1)} %get-tuple-element.39) | copy-start | bytes 1572868
  107.8 19.3 %collective-permute-start.21 = (bf16[8,256,128]{2,1,0:T(8,128)(2,1)S(1)}, bf16[8,256,128]{2,1,0:T(8,128)(2,1)S(1)}, u32[]{:S(2)}, u32[]{:S(2)}) collective-permute-start(bf16[8,256,128]{2,1,0:T(8,128)(2,1)S(1)} %add_convert_fusion.1), channel_id=1, source_target_pairs={{0,16},{8,24},{16,0},{24,8},{32,48},{40,56},{48,32},{56,40},{64,80... | collective-permute-start | bytes 1572872 | tf_op jit(solution)/shard_map/ppermute | solution.py:344
  114.8 34.3 %copy-start.4 = (bf16[3072,128]{1,0:T(8,128)(2,1)S(1)}, bf16[3072,128]{1,0:T(8,128)(2,1)}, u32[]{:S(2)}) copy-start(bf16[3072,128]{1,0:T(8,128)(2,1)} %get-tuple-element.41) | copy-start | bytes 2359300
  115.0 34.1 %collective-permute-start.15 = (bf16[3072,128]{1,0:T(8,128)(2,1)S(1)}, bf16[3072,128]{1,0:T(8,128)(2,1)S(1)}, u32[]{:S(2)}, u32[]{:S(2)}) collective-permute-start(bf16[3072,128]{1,0:T(8,128)(2,1)S(1)} %add_convert_fusion), channel_id=1, source_target_pairs={{64,0},{72,8},{80,16},{88,24},{96,32},{104,40},{112,48},{120,56},{... | collective-permute-start | bytes 2359304 | tf_op jit(solution)/shard_map/ppermute | solution.py:344
  127.1 23.3 %copy-start.9 = (bf16[8,256,128]{2,1,0:T(8,128)(2,1)}, bf16[8,256,128]{2,1,0:T(8,128)(2,1)S(1)}, u32[]{:S(2)}) copy-start(bf16[8,256,128]{2,1,0:T(8,128)(2,1)S(1)} %collective-permute-done.21) | copy-start | bytes 1572868
  127.2 15.6 %collective-permute-start.22 = (bf16[4,256,128]{2,1,0:T(8,128)(2,1)S(1)}, bf16[4,256,128]{2,1,0:T(8,128)(2,1)S(1)}, u32[]{:S(2)}, u32[]{:S(2)}) collective-permute-start(bf16[4,256,128]{2,1,0:T(8,128)(2,1)S(1)} %add_convert_fusion.2), channel_id=1, source_target_pairs={{0,32},{8,40},{16,48},{24,56},{32,0},{40,8},{48,16},{56,24},{64,96... | collective-permute-start | bytes 786440 | tf_op jit(solution)/shard_map/ppermute | solution.py:344
  138.4 26.2 %collective-permute-start.18 = (bf16[1024,128]{1,0:T(8,128)(2,1)}, bf16[1024,128]{1,0:T(8,128)(2,1)S(1)}, u32[]{:S(2)}, u32[]{:S(2)}) collective-permute-start(bf16[1024,128]{1,0:T(8,128)(2,1)} %add_convert_fusion.3), channel_id=1, source_target_pairs={{0,16},{8,24},{16,32},{24,40},{32,48},{40,56},{48,0},{56,8},{64,80... | collective-permute-start | bytes 786440 | tf_op jit(solution)/shard_map/ppermute | solution.py:344
  142.8 7.6 %copy-start.10 = (bf16[4,256,128]{2,1,0:T(8,128)(2,1)}, bf16[4,256,128]{2,1,0:T(8,128)(2,1)S(1)}, u32[]{:S(2)}) copy-start(bf16[4,256,128]{2,1,0:T(8,128)(2,1)S(1)} %collective-permute-done.22) | copy-start | bytes 786436
  142.9 13.9 %collective-permute-start.23 = (bf16[2,256,128]{2,1,0:T(8,128)(2,1)S(1)}, bf16[2,256,128]{2,1,0:T(8,128)(2,1)}, u32[]{:S(2)}, u32[]{:S(2)}) collective-permute-start(bf16[2,256,128]{2,1,0:T(8,128)(2,1)S(1)} %add_convert_fusion.6), channel_id=1, source_target_pairs={{0,64},{8,72},{16,80},{24,88},{32,96},{40,104},{48,112},{56,120},{... | collective-permute-start | bytes 393224 | tf_op jit(solution)/shard_map/ppermute | solution.py:344
  149.1 4.0 %copy-start.5 = (bf16[3072,128]{1,0:T(8,128)(2,1)}, bf16[3072,128]{1,0:T(8,128)(2,1)S(1)}, u32[]{:S(2)}) copy-start(bf16[3072,128]{1,0:T(8,128)(2,1)S(1)} %collective-permute-done.13) | copy-start | bytes 2359300
  149.1 4.0 %copy-start.6 = (bf16[3072,128]{1,0:T(8,128)(2,1)}, bf16[3072,128]{1,0:T(8,128)(2,1)S(1)}, u32[]{:S(2)}) copy-start(bf16[3072,128]{1,0:T(8,128)(2,1)S(1)} %collective-permute-done.15) | copy-start | bytes 2359300
  150.4 14.2 %collective-permute-start.17 = (bf16[1024,128]{1,0:T(8,128)(2,1)}, bf16[1024,128]{1,0:T(8,128)(2,1)S(1)}, u32[]{:S(2)}, u32[]{:S(2)}) collective-permute-start(bf16[1024,128]{1,0:T(8,128)(2,1)} %get-tuple-element.47), channel_id=1, source_target_pairs={{0,32},{8,40},{16,48},{24,56},{32,0},{40,8},{48,16},{56,24},{64,96... | collective-permute-start | bytes 786440 | tf_op jit(solution)/shard_map/ppermute | solution.py:344
  153.1 11.5 %collective-permute-start.16 = (bf16[1024,128]{1,0:T(8,128)(2,1)}, bf16[1024,128]{1,0:T(8,128)(2,1)S(1)}, u32[]{:S(2)}, u32[]{:S(2)}) collective-permute-start(bf16[1024,128]{1,0:T(8,128)(2,1)} %get-tuple-element.48), channel_id=1, source_target_pairs={{0,48},{8,56},{16,0},{24,8},{32,16},{40,24},{48,32},{56,40},{64,11... | collective-permute-start | bytes 786440 | tf_op jit(solution)/shard_map/ppermute | solution.py:344
  153.1 14.1 %copy-start.11 = (f32[512,128]{1,0:T(8,128)S(1)}, f32[512,128]{1,0:T(8,128)}, u32[]{:S(2)}) copy-start(f32[512,128]{1,0:T(8,128)} %get-tuple-element.37) | copy-start | bytes 786436
  153.1 14.1 %collective-permute-start.11 = (f32[512,128]{1,0:T(8,128)}, f32[512,128]{1,0:T(8,128)S(1)}, u32[]{:S(2)}, u32[]{:S(2)}) collective-permute-start(f32[512,128]{1,0:T(8,128)} %get-tuple-element.38), channel_id=1, source_target_pairs={{0,8},{8,0},{16,24},{24,16},{32,40},{40,32},{48,56},{56,48},{64,72... | collective-permute-start | bytes 786440 | tf_op jit(solution)/shard_map/ppermute | solution.py:344
  157.7 10.4 %collective-permute-start.24 = (bf16[1,256,128]{2,1,0:T(8,128)(2,1)S(1)}, bf16[1,256,128]{2,1,0:T(8,128)(2,1)S(1)}, u32[]{:S(2)}, u32[]{:S(2)}) collective-permute-start(bf16[1,256,128]{2,1,0:T(8,128)(2,1)S(1)} %add_convert_fusion.7), channel_id=1, source_target_pairs={{0,128},{8,136},{16,144},{24,152},{32,160},{40,168},{48,176},{56,1... | collective-permute-start | bytes 196616 | tf_op jit(solution)/shard_map/ppermute | solution.py:344
  166.0 11.6 %collective-permute-start.19 = (bf16[1024,128]{1,0:T(8,128)(2,1)S(1)}, bf16[1024,128]{1,0:T(8,128)(2,1)S(1)}, u32[]{:S(2)}, u32[]{:S(2)}) collective-permute-start(bf16[1024,128]{1,0:T(8,128)(2,1)S(1)} %fusion.7), channel_id=1, source_target_pairs={{64,0},{72,8},{80,16},{88,24},{96,32},{104,40},{112,48},{120,56},{... | collective-permute-start | bytes 786440 | tf_op jit(solution)/shard_map/ppermute | solution.py:344
Sparse Core Ops, SparseCore 0:
  9.8 58.3 all-gather.1
  76.2 70.7 reduce-scatter.1
where the time goes:
time: 190 us; the launch traced here: 186 us
  starting transfers between devices  58.5 us (31%)
  waiting for transfers between devices  50.7 us (27%)
  Pallas kernels  39 us (21%)
  other arithmetic  15.9 us (8%)
  between operations  14.5 us (8%)
  local copies, waits for them, and re-layouts  4.59 us (2%)
  matrix products  3.25 us (2%)
    ppermute x25, starting transfers between devices, send(): return lax.ppermute(value, 'ctx', pairs)  58.4 us
    ppermute x25, waiting for transfers between devices, send(): return lax.ppermute(value, 'ctx', pairs)  50 us
    pallas_call x3, Pallas kernels, bwd_call(): pl.pallas_call(functools.partial(bwd_body, base, plan, diag, first, last)...  14.2 us
    pallas_call x3, Pallas kernels, fwd_call(): pl.pallas_call(functools.partial(fwd_body, base, plan, diag, first, last)...  11.7 us
    pallas_call x1, Pallas kernels, wout_call(): pl.pallas_call(wout_body, grid_spec=pltpu.PrefetchScalarGridSpec(num_scal...  8.08 us
    convert_element_type x8, other arithmetic, bf(): return v.astype(BF16)  5.81 us
    pallas_call x1, Pallas kernels, grad_attn_call(): pl.pallas_call(grad_attn_body, grid=(cols // wide,), out_shape=jax.ShapeD...  5.06 us
  transfers between devices with their start and end apart: 27, of which 7 were waited for; matrix products, arithmetic and copies ran while one was open for 12% of the time, Pallas kernels for 21%

commit v1 on v0

v1 whole, which is shorter than its diff:
```python
import functools

import jax
import jax.numpy as jnp
from jax import lax
from jax.experimental import pallas as pl
from jax.experimental.pallas import tpu as pltpu
from jax.sharding import PartitionSpec as P

HEAD_SIZE = 128
BT = 512
KV = 2 * BT
NB = 32
SCALE = HEAD_SIZE**-0.5
LOG2E = 1.4426950408889634
C2 = SCALE * LOG2E
ROWS = 256
COLS = 512
F32 = jnp.float32
BF16 = jnp.bfloat16


VM = pl.BlockSpec(memory_space=pltpu.VMEM)
SM = pl.BlockSpec(memory_space=pltpu.SMEM)
ANY = pl.BlockSpec(memory_space=pl.ANY)


def dot_t(a, b):
    return lax.dot_general(a, b, (((1,), (1,)), ((), ())), preferred_element_type=F32)


def fetch(flags, base, sources, buf, sems):
    for e, (ref, row) in enumerate(sources):
        @pl.when(flags[2 * (base + e)] + flags[2 * (base + e) + 1] > 0)
        def _():
            pltpu.make_async_copy(ref.at[pl.ds(row, KV)], buf.at[e], sems.at[e]).start()


def walk(visit, n, diag):
    if diag:
        lax.fori_loop(0, 2, lambda i, carry: visit(True, i * diag, carry), 0)
        lax.fori_loop(0, n - 2, lambda i, carry: visit(False, jnp.where(i < diag - 1, i + 1, i + 2), carry), 0)
    else:
        lax.fori_loop(0, n, lambda i, carry: visit(False, i, carry), 0)


def fwd_body(base, plan, diag, first, last, *refs):
    n = len(plan)
    count = 1 + max(i for i, _ in plan)
    flags, q_ref = refs[0], refs[1]
    pos = 2
    if not first:
        ml_in, acc_in = refs[pos : pos + 2]
        pos += 2
    arrays = refs[pos : pos + count]
    pos += count
    if last:
        own_ref, sib_ref, lse_ref = refs[pos : pos + 3]
        pos += 3
    ml_ref, acc_ref, buf, sems = refs[pos : pos + 4]
    fetch(flags, base, [(arrays[i], row) for i, row in plan], buf, sems)
    if first:
        ml_ref[0] = jnp.full((2, BT), -jnp.inf, F32)
        ml_ref[1] = jnp.zeros((2, BT), F32)
        acc_ref[...] = jnp.zeros(acc_ref.shape, F32)
    else:
        ml_ref[...] = ml_in[...]
        acc_ref[...] = acc_in[...]

    def unit(e, h, masked):
        k = buf[e, :BT, :]
        v = buf[e, BT:, :]
        for r in range(0, BT, COLS):
            at = slice(r, r + COLS)
            s = dot_t(k, q_ref[h, at, :]) * C2
            if masked:
                row = lax.broadcasted_iota(jnp.int32, (BT, COLS), 0)
                col = lax.broadcasted_iota(jnp.int32, (BT, COLS), 1) + r
                near = jnp.where((e == 0) & (h == 0) | (e == diag) & (h == 1), 0, BT)
                s = jnp.where(row <= col + near, s, -jnp.inf)
            m_old = ml_ref[0, pl.ds(h, 1), at]
            m_new = jnp.maximum(m_old, jnp.max(s, axis=0, keepdims=True))
            alpha = jnp.exp2(m_old - m_new)
            p = jnp.exp2(s - m_new)
            ml_ref[0, pl.ds(h, 1), at] = m_new
            ml_ref[1, pl.ds(h, 1), at] = ml_ref[1, pl.ds(h, 1), at] * alpha + jnp.sum(p, axis=0, keepdims=True)
            acc_ref[h, :, at] = acc_ref[h, :, at] * alpha + lax.dot_general(
                v, p.astype(BF16), (((0,), (0,)), ((), ())), preferred_element_type=F32
            )

    def visit(masked, e, carry):
        @pl.when(flags[2 * (base + e)] + flags[2 * (base + e) + 1] > 0)
        def _():
            pltpu.make_async_copy(arrays[0].at[pl.ds(0, KV)], buf.at[e], sems.at[e]).wait()

            def one(h, c2):
                @pl.when(flags[2 * (base + e) + h] > 0)
                def _():
                    unit(e, h, masked)

                return c2

            lax.fori_loop(0, 2, one, 0)

        return carry

    walk(visit, n, diag)
    if last:
        lse_ref[...] = ml_ref[0] + jnp.log2(ml_ref[1])
        for h, ref in ((0, own_ref), (1, sib_ref)):
            ref[...] = jnp.transpose(acc_ref[h] / ml_ref[1, h : h + 1, :]).astype(BF16)


def fwd_call(flags, base, q2, state, arrays, plan, diag=0, last=False):
    n = len(plan)
    first = state is None
    shapes = ((2, 2, BT), (2, HEAD_SIZE, BT))
    scratch = [pltpu.VMEM((n, KV, HEAD_SIZE), BF16), pltpu.SemaphoreType.DMA((n,))]
    if last:
        out_shape = (
            jax.ShapeDtypeStruct((BT, HEAD_SIZE), BF16),
            jax.ShapeDtypeStruct((BT, HEAD_SIZE), BF16),
            jax.ShapeDtypeStruct((2, BT), F32),
        )
        scratch = [pltpu.VMEM(shape, F32) for shape in shapes] + scratch
    else:
        out_shape = tuple(jax.ShapeDtypeStruct(shape, F32) for shape in shapes)
    return pl.pallas_call(
        functools.partial(fwd_body, base, plan, diag, first, last),
        out_shape=out_shape,
        in_specs=[SM, VM] + ([] if first else [VM] * 2) + [ANY] * len(arrays),
        out_specs=tuple(VM for _ in out_shape),
        scratch_shapes=scratch,
        name="fwd",
        cost_estimate=pl.CostEstimate(flops=n * 268435456, transcendentals=n * 524288, bytes_accessed=n * 262144),
    )(flags, q2, *(() if first else state), *arrays)


def bwd_body(base, plan, diag, first, last, *refs):
    n = len(plan)
    half = n // 2
    count = 1 + max(i for i, _ in plan)
    flags, q_ref, do_own, do_sib, lse_ref = refs[:5]
    if first:
        own_ref, sib_ref = refs[5:7]
    else:
        dq_in, delta_in = refs[5:7]
    pos = 7
    arrays = refs[pos : pos + count]
    pos += count
    if last:
        dq_own, dq_sib = refs[pos : pos + 2]
        pos += 2
    else:
        dq_out, delta_out = refs[pos : pos + 2]
        pos += 2
    keep_ref, give_ref = refs[pos : pos + 2]
    pos += 2
    dq, delta_ref, do_ref, dkv, buf, obuf, sems, osems = refs[pos : pos + 8]
    fetch(flags, base, [(arrays[i], row) for i, row in plan], buf, sems)
    do_ref[0] = do_own[...]
    do_ref[1] = do_sib[...]
    if first:
        dq[...] = jnp.zeros(dq.shape, F32)
        for h, ref in ((0, own_ref), (1, sib_ref)):
            prod = do_ref[h].astype(F32) * ref[...].astype(F32)
            delta_ref[h : h + 1, :] = jnp.sum(jnp.transpose(prod), axis=0, keepdims=True)
    else:
        dq[...] = dq_in[...]
        delta_ref[...] = delta_in[...]

    def unit(e, h, masked):
        q = q_ref[h]
        do = do_ref[h]
        lse = lse_ref[pl.ds(h, 1), :]
        delta = delta_ref[pl.ds(h, 1), :]
        for r in range(0, BT, ROWS):
            at = slice(r, r + ROWS)
            vt = slice(BT + r, BT + r + ROWS)
            k = buf[e, at, :]
            p = jnp.exp2(dot_t(k, q) * C2 - lse)
            if masked:
                row = lax.broadcasted_iota(jnp.int32, (ROWS, BT), 0) + r
                col = lax.broadcasted_iota(jnp.int32, (ROWS, BT), 1)
                near = jnp.where((e == 0) & (h == 0) | (e == diag) & (h == 1), 0, BT)
                p = jnp.where(row <= col + near, p, 0.0)
            ds = (p * (dot_t(buf[e, vt, :], do) - delta) * SCALE).astype(BF16)
            dkv[vt, :] += jnp.dot(p.astype(BF16), do, preferred_element_type=F32)
            dkv[at, :] += jnp.dot(ds, q, preferred_element_type=F32)
            dq[h] += lax.dot_general(k, ds, (((0,), (0,)), ((), ())), preferred_element_type=F32)

    def visit(masked, e, carry):
        on = flags[2 * (base + e)] + flags[2 * (base + e) + 1] > 0

        @pl.when(on)
        def _():
            pltpu.make_async_copy(arrays[0].at[pl.ds(0, KV)], buf.at[e], sems.at[e]).wait()
            dkv[...] = jnp.zeros(dkv.shape, F32)

            def one(h, c2):
                @pl.when(flags[2 * (base + e) + h] > 0)
                def _():
                    unit(e, h, masked)

                return c2

            lax.fori_loop(0, 2, one, 0)
            obuf[e] = dkv[...].astype(BF16)

        @pl.when(jnp.logical_not(on))
        def _():
            obuf[e] = jnp.zeros((KV, HEAD_SIZE), BF16)

        @pl.when(e < half)
        def _():
            pltpu.make_async_copy(obuf.at[e], keep_ref.at[pl.ds(e * KV, KV)], osems.at[e]).start()

        @pl.when(e >= half)
        def _():
            pltpu.make_async_copy(obuf.at[e], give_ref.at[pl.ds((e - half) * KV, KV)], osems.at[e]).start()

        return carry

    walk(visit, n, diag)
    if last:
        dq_own[...] = jnp.transpose(dq[0])
        dq_sib[...] = jnp.transpose(dq[1])
    else:
        dq_out[...] = dq[...]
        delta_out[...] = delta_ref[...]
    for e in range(n):
        pltpu.make_async_copy(obuf.at[e], keep_ref.at[pl.ds(0, KV)], osems.at[e]).wait()


def bwd_call(flags, base, q2, do_own, do_sib, lse, state, arrays, plan, diag=0, first=False, last=False):
    n = len(plan)
    dq_shape = (2, HEAD_SIZE, BT)
    head = jax.ShapeDtypeStruct((BT, HEAD_SIZE), F32)
    dq_outs = (head, head) if last else (jax.ShapeDtypeStruct(dq_shape, F32), jax.ShapeDtypeStruct((2, BT), F32))
    part = jax.ShapeDtypeStruct((n // 2 * KV, HEAD_SIZE), BF16)
    return pl.pallas_call(
        functools.partial(bwd_body, base, plan, diag, first, last),
        out_shape=dq_outs + (part, part),
        in_specs=[SM] + [VM] * 6 + [ANY] * len(arrays),
        out_specs=(VM,) * len(dq_outs) + (ANY, ANY),
        scratch_shapes=[
            pltpu.VMEM(dq_shape, F32),
            pltpu.VMEM((2, BT), F32),
            pltpu.VMEM((2, BT, HEAD_SIZE), BF16),
            pltpu.VMEM((KV, HEAD_SIZE), F32),
            pltpu.VMEM((n, KV, HEAD_SIZE), BF16),
            pltpu.VMEM((n, KV, HEAD_SIZE), BF16),
            pltpu.SemaphoreType.DMA((n,)),
            pltpu.SemaphoreType.DMA((n,)),
        ],
        name="bwd",
        cost_estimate=pl.CostEstimate(flops=n * 671088640, transcendentals=n * 524288, bytes_accessed=n * 524288),
    )(flags, q2, do_own, do_sib, lse, *state, *arrays)


ORDER = (0, 2, 1, 3)


def order(i):
    return (i % 2) * 2 + i // 2


def grads_body(where_ref, a_ref, *refs):
    pieces, weights = refs[:4], refs[4:8]
    keep_ref, give_ref, mine_ref, other_ref, at, acc = refs[8:]
    step = pl.program_id(0)

    @pl.when(step == 0)
    def _():
        at[...] = jnp.transpose(a_ref[...])
        acc[...] = jnp.zeros(acc.shape, F32)

    first = where_ref[2] == 0
    total = acc[...]
    for i in range(4):
        piece = pieces[i][...]
        total = total + dot_t(piece, weights[i][...])
        term = jnp.dot(at[...], piece, preferred_element_type=F32).astype(BF16)
        keep_ref[i] = jnp.where(first, term[:, :128], term[:, 128:])
        give_ref[i] = jnp.where(first, term[:, 128:], term[:, :128])
    acc[...] = total

    @pl.when(step == pl.num_programs(0) - 1)
    def _():
        low = total.astype(BF16)
        mine_ref[...] = jnp.where(first, low[:, :128], low[:, 128:])
        other_ref[...] = jnp.where(first, low[:, 128:], low[:, :128])


def grads_call(where, attn, piece, w_out):
    rows, width = attn.shape

    def column(i):
        return lambda p, w: (0, 4 * (w[0] ^ ORDER[i]) + (w[1] ^ order(p)))

    out = jax.ShapeDtypeStruct((16, width, 128), BF16)
    spec = pl.BlockSpec((4, width, 128), lambda p, w: (p, 0, 0))
    return pl.pallas_call(
        grads_body,
        grid_spec=pltpu.PrefetchScalarGridSpec(
            num_scalar_prefetch=1,
            grid=(4,),
            in_specs=[pl.BlockSpec((rows, width), lambda p, w: (0, 0))]
            + [pl.BlockSpec((rows, 256), column(i)) for i in range(4)]
            + [pl.BlockSpec((width, 256), column(i)) for i in range(4)],
            out_specs=[spec, spec] + [pl.BlockSpec((rows, HEAD_SIZE), lambda p, w: (0, 0))] * 2,
            scratch_shapes=[pltpu.VMEM((width, rows), BF16), pltpu.VMEM((rows, width), F32)],
        ),
        out_shape=(out, out) + (jax.ShapeDtypeStruct((rows, HEAD_SIZE), BF16),) * 2,
        name="grads",
        cost_estimate=pl.CostEstimate(flops=2147483648, transcendentals=0, bytes_accessed=8912896),
    )(where, attn, *([piece] * 4), *([w_out] * 4))


def send(value, rule):
    pairs = []
    for b in range(NB):
        to = rule(b // 8, b // 2 % 4, b % 2)
        if to is not None:
            x, y, c = to
            pairs.append((b, 8 * x + 2 * y + c))
    return lax.ppermute(value, "ctx", pairs)


def swap(value):
    return send(value, lambda x, y, c: (x, y, 1 - c))


def ahead(value):
    return send(value, lambda x, y, c: (x + 1, y, c) if x < 3 else None)


def back(value):
    return send(value, lambda x, y, c: (x - 1, y, c) if x > 0 else None)


def along(value, k):
    return send(value, lambda x, y, c: (x, (y + k) % 4, c))


def bf(v):
    return v.astype(BF16)


def f32(v):
    return v.astype(F32)


def per_device(query_proj, projected_keys, projected_values, w_out, attended_blocks, grad_out):
    rank = lax.axis_index("ctx")
    x, y, c = rank // 8, rank // 2 % 4, rank % 2
    sib = rank + 1 - 2 * c

    piece = lax.all_gather(grad_out, "head", axis=1, tiled=True)

    def mine_of(v):
        return jnp.where(c == 0, v[:, :HEAD_SIZE], v[:, HEAD_SIZE:])

    def other_of(v):
        return jnp.where(c == 0, v[:, HEAD_SIZE:], v[:, :HEAD_SIZE])

    def joined(own, other):
        return jnp.where(c == 0, jnp.concatenate([own, other], 1), jnp.concatenate([other, own], 1))

    own = jnp.concatenate([projected_keys, projected_values], 0)
    x1 = ahead(own)
    ownx = swap(jnp.concatenate([projected_keys, projected_values, other_of(query_proj)], 0))
    d1 = along(jnp.where(y < 3, own, x1), 1)
    d2 = along(jnp.where(y < 2, own, x1), 2)
    d3 = along(jnp.where(y < 1, own, x1), 3)
    d8 = ahead(x1)
    x1x = swap(x1)
    pre = jnp.concatenate([d1, d2], 0)
    far = ahead(pre)
    prex = swap(pre)
    d3x = swap(d3)
    d8x = swap(d8)
    farx = swap(far)
    q2 = jnp.stack([mine_of(query_proj), ownx[KV:]])

    keys = jnp.concatenate([b - 2 * jnp.array(d) for d in ([0], [1, 2, 4, 3], [5, 6, 8]) for b in (rank, sib)])
    lists = jnp.stack(
        [lax.dynamic_index_in_dim(attended_blocks, r, 0, keepdims=False) for r in (rank, sib)]
    )
    hit = jnp.any(lists[None] == keys[:, None, None], -1) & (keys >= 0)[:, None]
    flags = hit.astype(jnp.int32).reshape(-1)
    self_blocks = ([own, ownx], ((0, 0), (1, 0)))
    near_blocks = ([pre, x1, d3, prex, x1x, d3x], ((0, 0), (0, KV), (1, 0), (2, 0), (3, 0), (3, KV), (4, 0), (5, 0)))
    far_blocks = ([far, d8, farx, d8x], ((0, 0), (0, KV), (1, 0), (2, 0), (2, KV), (3, 0)))
    state = fwd_call(flags, 0, q2, None, *self_blocks, diag=1)
    state = fwd_call(flags, 2, q2, state, *near_blocks)
    attn_own, attn_sib, lse = fwd_call(flags, 10, q2, state, *far_blocks, last=True)
    attn_other = swap(attn_sib)
    attn = joined(attn_own, attn_other)

    out_terms = bf(jnp.dot(attn, w_out, preferred_element_type=F32))
    layer_out = lax.psum_scatter(out_terms, "head", scatter_dimension=1, tiled=True)
    wkeep, wgive, do_own, do_other = grads_call(jnp.stack([x, y, c]), attn, piece, w_out)
    do_sib = swap(do_other)
    wcame = swap(wgive)

    def summed(n, parts, sent):
        low, high = [p[:n] for p in parts] + [sent[:n]], [p[n : 2 * n] for p in parts] + [sent[n : 2 * n]]
        return low, bf(sum(f32(p) for p in high))

    args = (q2, do_own, do_sib, lse)
    dq, delta, keep, give = bwd_call(flags, 10, *args, (attn_own, attn_sib), *far_blocks, first=True)
    got = swap(give)
    came = back(bf(f32(keep) + f32(got)))
    parts, gave = summed(8, [wkeep], wcame)
    wcame = send(gave, lambda x, y, c: (x, y ^ 1, c))
    dq, delta, keep, give = bwd_call(flags, 2, *args, (dq, delta), *near_blocks)
    got = swap(give)
    dq_own, dq_sib, keep0, give0 = bwd_call(flags, 0, *args, (dq, delta), *self_blocks, diag=1, last=True)
    got0 = swap(give0)
    dq_other = swap(dq_sib)
    parts, gave = summed(4, parts, wcame)
    wcame = send(gave, lambda x, y, c: (x, y ^ 2, c))
    t1, t2, t4 = [f32(keep[at]) + f32(got[at]) + f32(came[at]) for at in (slice(i, i + KV) for i in (0, KV, 2 * KV))]
    t3 = f32(keep[3 * KV :]) + f32(got[3 * KV :])
    s1 = along(bf(t1), -1)
    s2 = along(bf(t2), -2)
    s3 = along(bf(t3), -3)
    parts, gave = summed(2, parts, wcame)
    wcame = send(gave, lambda x, y, c: (x ^ 1, y, c))

    def kept(cond, v):
        return jnp.where(cond, f32(v), 0.0)

    r4 = back(bf(t4 + kept(y == 3, s1) + kept(y >= 2, s2) + kept(y >= 1, s3)))
    parts, gave = summed(1, parts, wcame)
    wcame = send(gave, lambda x, y, c: (x ^ 2, y, c))
    grad_wout = sum(f32(p[0]) for p in parts) + f32(wcame[0])
    grad_query = joined(dq_own, dq_other)
    total = f32(keep0) + f32(got0) + kept(y < 3, s1) + kept(y < 2, s2) + kept(y < 1, s3)
    total = lax.optimization_barrier(total)
    grad_key, grad_value = [total[at] + f32(r4[at]) for at in (slice(0, BT), slice(BT, KV))]
    return (layer_out, grad_query, grad_key, grad_value, grad_wout)


def solution(mesh):
    return jax.shard_map(
        per_device,
        mesh=mesh,
        in_specs=(
            P("ctx", "head"),
            P("ctx", "head"),
            P("ctx", "head"),
            P("head", None),
            P(),
            P("ctx", "head"),
        ),
        out_specs=(
            P("ctx", "head"),
            P("ctx", "head"),
            P("ctx", "head"),
            P("ctx", "head"),
            P("head", "ctx"),
        ),
        check_vma=False,
    )
```

time: 190 us -> 176 us (0.926)
  waiting for transfers between devices: 50.7 us -> 38.9 us
  Pallas kernels: 39 us -> 31.1 us
  starting transfers between devices: 58.5 us -> 64.5 us
    ppermute x25 -> x28, waiting for transfers between devices: 50 us -> 38.2 us  [send(): return lax.ppermute(value, 'ctx', pairs)]
    ppermute x25 -> x28, starting transfers between devices: 58.4 us -> 64.4 us  [send(): return lax.ppermute(value, 'ctx', pairs)]
    pallas_call x2 -> x1, Pallas kernels: 13.1 us -> 7.49 us  [grads_call(): pl.pallas_call(grads_body, grid_spec=pltpu.PrefetchScalarGridSpec(num_sca...]
    convert_element_type x8 -> x7, other arithmetic: 5.81 us -> 8.3 us  [bf(): return v.astype(BF16)]
    pallas_call x3, Pallas kernels: 11.7 us -> 9.38 us  [fwd_call(): pl.pallas_call(functools.partial(fwd_body, base, plan, diag, first, last)...]
  transfers between devices with their start and end apart: 27 -> 30, of which waited for: 7 -> 8; matrix products, arithmetic and copies ran while one was open for 12% -> 13% of each run, Pallas kernels for 21% -> 18%
where the time goes in v1:
time: 176 us; the launch traced here: 174 us
  starting transfers between devices  64.5 us (37%)
  waiting for transfers between devices  38.9 us (22%)
  Pallas kernels  31.1 us (18%)
  other arithmetic  16.3 us (9%)
  between operations  14.5 us (8%)
  local copies, waits for them, and re-layouts  5.23 us (3%)
  matrix products  3.26 us (2%)
    ppermute x28, starting transfers between devices, send(): return lax.ppermute(value, 'ctx', pairs)  64.4 us
    ppermute x28, waiting for transfers between devices, send(): return lax.ppermute(value, 'ctx', pairs)  38.2 us
    pallas_call x3, Pallas kernels, bwd_call(): pl.pallas_call(functools.partial(bwd_body, base, plan, diag, first, last)...  14.2 us
    pallas_call x3, Pallas kernels, fwd_call(): pl.pallas_call(functools.partial(fwd_body, base, plan, diag, first, last)...  9.38 us
    convert_element_type x7, other arithmetic, bf(): return v.astype(BF16)  8.3 us
    pallas_call x1, Pallas kernels, grads_call(): pl.pallas_call(grads_body, grid_spec=pltpu.PrefetchScalarGridSpec(num_sca...  7.49 us
  transfers between devices with their start and end apart: 30, of which 8 were waited for; matrix products, arithmetic and copies ran while one was open for 13% of the time, Pallas kernels for 18%

profile of v1, /device:TPU:1, one launch (start us, length us, event | category | flops | bytes accessed | tf_op | source)
XLA Modules:
  0.0 173.7 jit_solution(6158436729726134059)
XLA Ops:
  8.0 0.9 constant_dynamic-update-slice_fusion.1
  8.9 0.9 constant_dynamic-update-slice_fusion.refs_2_.refs_7_
  9.8 3.9 %collective-permute-start.1 = (bf16[1024,128]{1,0:T(8,128)(2,1)S(1)}, bf16[1024,128]{1,0:T(8,128)(2,1)S(1)}, u32[]{:S(2)}, u32[]{:S(2)}) collective-permute-start(bf16[1024,128]{1,0:T(8,128)(2,1)S(1)} %constant_dynamic-update-slice_fusion.refs_2_.refs_7_), channel_id=1, source_target_pairs={{0,64},{8,72},{16,80},{24,88},{32,96},{40,104},{48,112},{56,120},{... | collective-permute-start | bytes 786440 | tf_op jit(solution)/shard_map/ppermute | solution.py:327
  13.8 1.0 select_bitcast_fusion
  14.8 1.0 pad_maximum_fusion
  15.8 1.0 collective-permute-start
  16.9 1.9 %collective-permute-done.1.refs_5_.refs_8_ = bf16[1024,128]{1,0:T(8,128)(2,1)S(1)} collective-permute-done((bf16[1024,128]{1,0:T(8,128)(2,1)S(1)}, bf16[1024,128]{1,0:T(8,128)(2,1)S(1)}, u32[]{:S(2)}, u32[]{:S(2)}) %collective-permute-start.1) | collective-permute-done | bytes 262176 | tf_op jit(solution)/shard_map/ppermute | solution.py:327
  18.8 1.4 collective-permute-start.2
  20.3 2.6 %collective-permute-start.3 = (bf16[1024,128]{1,0:T(8,128)(2,1)S(1)}, bf16[1024,128]{1,0:T(8,128)(2,1)S(1)}, u32[]{:S(2)}, u32[]{:S(2)}) collective-permute-start(bf16[1024,128]{1,0:T(8,128)(2,1)S(1)} %get-tuple-element.59), channel_id=1, source_target_pairs={{0,32},{8,40},{16,48},{24,56},{32,0},{40,8},{48,16},{56,24},{64,96... | collective-permute-start | bytes 786440 | tf_op jit(solution)/shard_map/ppermute | solution.py:327
  22.9 3.6 %collective-permute-done.2 = bf16[1024,128]{1,0:T(8,128)(2,1)S(1)} collective-permute-done((bf16[1024,128]{1,0:T(8,128)(2,1)S(1)}, bf16[1024,128]{1,0:T(8,128)(2,1)S(1)}, u32[]{:S(2)}, u32[]{:S(2)}) %collective-permute-start.2) | collective-permute-done | bytes 262176 | tf_op jit(solution)/shard_map/ppermute | solution.py:327
  26.6 6.7 %collective-permute-done.3 = bf16[1024,128]{1,0:T(8,128)(2,1)S(1)} collective-permute-done((bf16[1024,128]{1,0:T(8,128)(2,1)S(1)}, bf16[1024,128]{1,0:T(8,128)(2,1)S(1)}, u32[]{:S(2)}, u32[]{:S(2)}) %collective-permute-start.3) | collective-permute-done | bytes 262176 | tf_op jit(solution)/shard_map/ppermute | solution.py:327
  33.3 4.1 %collective-permute-start.8 = (bf16[2048,128]{1,0:T(8,128)(2,1)S(1)}, bf16[2048,128]{1,0:T(8,128)(2,1)S(1)}, u32[]{:S(2)}, u32[]{:S(2)}) collective-permute-start(bf16[2048,128]{1,0:T(8,128)(2,1)S(1)} %constant_dynamic-update-slice_fusion.2.refs_4_.refs_7_), channel_id=1, source_target_pairs={{0,64},{8,72},{16,80},{24,88},{32,96},{40,104},{48,112},{56,120},{... | collective-permute-start | bytes 1572872 | tf_op jit(solution)/shard_map/ppermute | solution.py:327
  37.9 3.8 %collective-permute-start.9 = (bf16[1024,128]{1,0:T(8,128)(2,1)S(1)}, bf16[1024,128]{1,0:T(8,128)(2,1)}, u32[]{:S(2)}, u32[]{:S(2)}) collective-permute-start(bf16[1024,128]{1,0:T(8,128)(2,1)S(1)} %collective-permute-done.1.refs_5_.refs_8_), channel_id=1, source_target_pairs={{0,64},{8,72},{16,80},{24,88},{32,96},{40,104},{48,112},{56,120},{... | collective-permute-start | bytes 786440 | tf_op jit(solution)/shard_map/ppermute | solution.py:327
  41.7 2.9 %collective-permute-start.5 = (bf16[2048,128]{1,0:T(8,128)(2,1)S(1)}, bf16[2048,128]{1,0:T(8,128)(2,1)S(1)}, u32[]{:S(2)}, u32[]{:S(2)}) collective-permute-start(bf16[2048,128]{1,0:T(8,128)(2,1)S(1)} %constant_dynamic-update-slice_fusion.2.refs_4_.refs_7_), channel_id=1, source_target_pairs={{0,8},{8,0},{16,24},{24,16},{32,40},{40,32},{48,56},{56,48},{64,72... | collective-permute-start | bytes 1572872 | tf_op jit(solution)/shard_map/ppermute | solution.py:327
  45.5 1.4 collective-permute-start.7
  46.9 5.5 %collective-permute-start.10 = (bf16[2048,128]{1,0:T(8,128)(2,1)S(1)}, bf16[2048,128]{1,0:T(8,128)(2,1)S(1)}, u32[]{:S(2)}, u32[]{:S(2)}) collective-permute-start(bf16[2048,128]{1,0:T(8,128)(2,1)S(1)} %collective-permute-done.8.refs_4_.refs_7_), channel_id=1, source_target_pairs={{0,8},{8,0},{16,24},{24,16},{32,40},{40,32},{48,56},{56,48},{64,72... | collective-permute-start | bytes 1572872 | tf_op jit(solution)/shard_map/ppermute | solution.py:327
  52.4 2.8 %collective-permute-start.11 = (bf16[1024,128]{1,0:T(8,128)(2,1)}, bf16[1024,128]{1,0:T(8,128)(2,1)}, u32[]{:S(2)}, u32[]{:S(2)}) collective-permute-start(bf16[1024,128]{1,0:T(8,128)(2,1)} %collective-permute-done.9.refs_5_.refs_8_), channel_id=1, source_target_pairs={{0,8},{8,0},{16,24},{24,16},{32,40},{40,32},{48,56},{56,48},{64,72... | collective-permute-start | bytes 786440 | tf_op jit(solution)/shard_map/ppermute | solution.py:327
  55.9 4.9 %fwd.3 = (f32[2,2,512]{2,1,0:T(2,128)}, f32[2,128,512]{2,1,0:T(8,128)}) custom-call(s32[32]{0:T(128)} %reshape.72.refs_0_, bf16[2,512,128]{2,1,0:T(8,128)(2,1)} %pad_maximum_fusion.1.refs_1_, bf16[1024,128]{1,0:T(8,128)(2,1)} %copy-done.5, bf16[1536,128]{1,0:T(8,128)(2,1)} %copy-done.11), custom_call_target="tpu_custom_call" | custom-call | flops 536870912 | bytes 524288 | tf_op jit(solution)/shard_map/fwd/pallas_call | solution.py:128
  61.7 2.2 %fwd.4 = (f32[2,2,512]{2,1,0:T(2,128)}, f32[2,128,512]{2,1,0:T(8,128)}) custom-call(s32[32]{0:T(128)} %reshape.72.refs_0_, bf16[2,512,128]{2,1,0:T(8,128)(2,1)} %pad_maximum_fusion.1.refs_1_, f32[2,2,512]{2,1,0:T(2,128)} %get-tuple-element.28.refs_2_, f32[2,128,512]{2,1,0:T(8,128)} %get-tuple-element.29.refs_3_, bf16[2048,128]{1,0:T(8,128)(2,1)} %copy-done.10, ...), custom_call_target="tpu_custom_call" | custom-call | flops 2147483648 | bytes 2097152 | tf_op jit(solution)/shard_map/fwd/pallas_call | solution.py:128
  64.7 2.3 %fwd.5 = (bf16[512,128]{1,0:T(8,128)(2,1)}, bf16[512,128]{1,0:T(8,128)(2,1)}, f32[2,512]{1,0:T(2,128)}) custom-call(s32[32]{0:T(128)} %reshape.72.refs_0_, bf16[2,512,128]{2,1,0:T(8,128)(2,1)} %pad_maximum_fusion.1.refs_1_, f32[2,2,512]{2,1,0:T(2,128)} %get-tuple-element.30.refs_2_, f32[2,128,512]{2,1,0:T(8,128)} %get-tuple-element.31.refs_3_, ...), custom_call_target="tpu_custom_call" | custom-call | flops 1610612736 | bytes 1572864 | tf_op jit(solution)/shard_map/fwd/pallas_call | solution.py:128
  67.1 1.5 collective-permute-done.12
  68.7 1.1 maximum_select_fusion.1.a_ref
  69.7 3.3 %convolution_convert_fusion = bf16[512,4096]{1,0:T(8,128)(2,1)} fusion(bf16[512,256]{1,0:T(8,128)(2,1)S(1)} %maximum_select_fusion.1.a_ref, bf16[256,4096]{1,0:T(8,128)(2,1)S(1)} %copy-done), kind=kOutput, calls=%fused_computation | convolution fusion | flops 1075838976 | bytes 6553600 | tf_op jit(solution)/shard_map/dot_general | solution.py:401
  73.7 7.5 %grads.1 = (bf16[16,256,128]{2,1,0:T(8,128)(2,1)}, bf16[16,256,128]{2,1,0:T(8,128)(2,1)}, bf16[512,128]{1,0:T(8,128)(2,1)}, bf16[512,128]{1,0:T(8,128)(2,1)}) custom-call(s32[3]{0:T(128)} %pad_add_fusion.1.where_ref, bf16[512,256]{1,0:T(8,128)(2,1)} %copy-done.1, bf16[512,4096]{1,0:T(8,128)(2,1)} %all-gather.2.cloned.1.call-done.refs_0_.refs_1_.refs_2_.refs_3_, ...), custom_call_target="tpu_custom_call" | custom-call | flops 2147483648 | bytes 8912896 | tf_op jit(solution)/shard_map/grads/pallas_call | solution.py:303
  81.8 2.5 %collective-permute-done.13.refs_3_ = bf16[512,128]{1,0:T(8,128)(2,1)S(1)} collective-permute-done((bf16[512,128]{1,0:T(8,128)(2,1)}, bf16[512,128]{1,0:T(8,128)(2,1)S(1)}, u32[]{:S(2)}, u32[]{:S(2)}) %collective-permute-start.13) | collective-permute-done | bytes 131104 | tf_op jit(solution)/shard_map/ppermute | solution.py:327
  85.0 3.5 %bwd.3 = (f32[2,128,512]{2,1,0:T(8,128)}, f32[2,512]{1,0:T(2,128)}, bf16[3072,128]{1,0:T(8,128)(2,1)}, bf16[3072,128]{1,0:T(8,128)(2,1)}) custom-call(s32[32]{0:T(128)} %reshape.72.refs_0_, bf16[2,512,128]{2,1,0:T(8,128)(2,1)} %pad_maximum_fusion.1.refs_1_, bf16[512,128]{1,0:T(8,128)(2,1)} %get-tuple-element.34.refs_2_, bf16[512,128]{1,0:T(8,128)(2,1)} %copy-done.18, ...), custom_call_target="tpu_custom_call" | custom-call | flops 4026531840 | bytes 3145728 | tf_op jit(solution)/shard_map/bwd/pallas_call | solution.py:241
  88.7 3.8 %bwd.4 = (f32[2,128,512]{2,1,0:T(8,128)}, f32[2,512]{1,0:T(2,128)}, bf16[4096,128]{1,0:T(8,128)(2,1)}, bf16[4096,128]{1,0:T(8,128)(2,1)}) custom-call(s32[32]{0:T(128)} %reshape.72.refs_0_, bf16[2,512,128]{2,1,0:T(8,128)(2,1)} %pad_maximum_fusion.1.refs_1_, bf16[512,128]{1,0:T(8,128)(2,1)} %get-tuple-element.34.refs_2_, bf16[512,128]{1,0:T(8,128)(2,1)} %copy-done.18, ...), custom_call_target="tpu_custom_call" | custom-call | flops 5368709120 | bytes 4194304 | tf_op jit(solution)/shard_map/bwd/pallas_call | solution.py:241
  93.2 2.1 %collective-permute-start.24 = (bf16[8,256,128]{2,1,0:T(8,128)(2,1)S(1)}, bf16[8,256,128]{2,1,0:T(8,128)(2,1)S(1)}, u32[]{:S(2)}, u32[]{:S(2)}) collective-permute-start(bf16[8,256,128]{2,1,0:T(8,128)(2,1)S(1)} %add_convert_fusion.1), channel_id=1, source_target_pairs={{0,16},{8,24},{16,0},{24,8},{32,48},{40,56},{48,32},{56,40},{64,80... | collective-permute-start | bytes 1572872 | tf_op jit(solution)/shard_map/ppermute | solution.py:327
  95.3 1.1 add_convert_fusion
  96.5 1.3 collective-permute-start.18
  97.7 9.8 %collective-permute-done.24 = bf16[8,256,128]{2,1,0:T(8,128)(2,1)S(1)} collective-permute-done((bf16[8,256,128]{2,1,0:T(8,128)(2,1)S(1)}, bf16[8,256,128]{2,1,0:T(8,128)(2,1)S(1)}, u32[]{:S(2)}, u32[]{:S(2)}) %collective-permute-start.24) | collective-permute-done | bytes 524320 | tf_op jit(solution)/shard_map/ppermute | solution.py:327
  107.6 0.9 add_convert_fusion.2
  108.5 8.8 %collective-permute-start.25 = (bf16[4,256,128]{2,1,0:T(8,128)(2,1)}, bf16[4,256,128]{2,1,0:T(8,128)(2,1)}, u32[]{:S(2)}, u32[]{:S(2)}) collective-permute-start(bf16[4,256,128]{2,1,0:T(8,128)(2,1)} %add_convert_fusion.2), channel_id=1, source_target_pairs={{0,32},{8,40},{16,48},{24,56},{32,0},{40,8},{48,16},{56,24},{64,96... | collective-permute-start | bytes 786440 | tf_op jit(solution)/shard_map/ppermute | solution.py:327
  117.3 6.8 %bwd.5 = (f32[512,128]{1,0:T(8,128)}, f32[512,128]{1,0:T(8,128)}, bf16[1024,128]{1,0:T(8,128)(2,1)}, bf16[1024,128]{1,0:T(8,128)(2,1)}) custom-call(s32[32]{0:T(128)} %reshape.72.refs_0_, bf16[2,512,128]{2,1,0:T(8,128)(2,1)} %pad_maximum_fusion.1.refs_1_, bf16[512,128]{1,0:T(8,128)(2,1)} %get-tuple-element.34.refs_2_, bf16[512,128]{1,0:T(8,128)(2,1)} %copy-done.18, ...), custom_call_target="tpu_custom_call" | custom-call | flops 1342177280 | bytes 1048576 | tf_op jit(solution)/shard_map/bwd/pallas_call | solution.py:241
  124.2 1.3 collective-permute-start.15
  125.4 1.0 add_convert_fusion.6
  126.5 8.0 %collective-permute-start.26 = (bf16[2,256,128]{2,1,0:T(8,128)(2,1)S(1)}, bf16[2,256,128]{2,1,0:T(8,128)(2,1)}, u32[]{:S(2)}, u32[]{:S(2)}) collective-permute-start(bf16[2,256,128]{2,1,0:T(8,128)(2,1)S(1)} %add_convert_fusion.6), channel_id=1, source_target_pairs={{0,64},{8,72},{16,80},{24,88},{32,96},{40,104},{48,112},{56,120},{... | collective-permute-start | bytes 393224 | tf_op jit(solution)/shard_map/ppermute | solution.py:327
  134.4 2.4 %add_convert_fusion.4 = (bf16[1024,128]{1,0:T(8,128)(2,1)}, bf16[1024,128]{1,0:T(8,128)(2,1)}, bf16[1024,128]{1,0:T(8,128)(2,1)}) fusion(bf16[3072,128]{1,0:T(8,128)(2,1)} %collective-permute-done.18, bf16[4096,128]{1,0:T(8,128)(2,1)} %collective-permute-done.16, bf16[4096,128]{1,0:T(8,128)(2,1)S(1)} %copy-done.3), kind=kLoop, calls=%fused_computation.19 | loop fusion | flops 2097152 | bytes 2883584 | tf_op jit(solution)/shard_map/convert_element_type | solution.py:347
  137.1 0.9 collective-permute-start.20
  138.6 3.2 %collective-permute-start.14 = (f32[512,128]{1,0:T(8,128)}, f32[512,128]{1,0:T(8,128)S(1)}, u32[]{:S(2)}, u32[]{:S(2)}) collective-permute-start(f32[512,128]{1,0:T(8,128)} %get-tuple-element.42), channel_id=1, source_target_pairs={{0,8},{8,0},{16,24},{24,16},{32,40},{40,32},{48,56},{56,48},{64,72... | collective-permute-start | bytes 786440 | tf_op jit(solution)/shard_map/ppermute | solution.py:327
  141.8 0.9 add_convert_fusion.7
  142.8 5.7 %collective-permute-start.27 = (bf16[1,256,128]{2,1,0:T(8,128)(2,1)S(1)}, bf16[1,256,128]{2,1,0:T(8,128)(2,1)S(1)}, u32[]{:S(2)}, u32[]{:S(2)}) collective-permute-start(bf16[1,256,128]{2,1,0:T(8,128)(2,1)S(1)} %add_convert_fusion.7), channel_id=1, source_target_pairs={{0,128},{8,136},{16,144},{24,152},{32,160},{40,168},{48,176},{56,1... | collective-permute-start | bytes 196616 | tf_op jit(solution)/shard_map/ppermute | solution.py:327
  148.5 4.0 %collective-permute-done.21 = bf16[1024,128]{1,0:T(8,128)(2,1)} collective-permute-done((bf16[1024,128]{1,0:T(8,128)(2,1)}, bf16[1024,128]{1,0:T(8,128)(2,1)}, u32[]{:S(2)}, u32[]{:S(2)}) %collective-permute-start.21) | collective-permute-done | bytes 262176 | tf_op jit(solution)/shard_map/ppermute | solution.py:327
  152.6 1.8 %fusion.6 = (bf16[1024,128]{1,0:T(8,128)(2,1)S(1)}, f32[1024,128]{1,0:T(8,128)S(1)}) fusion(bf16[1024,128]{1,0:T(8,128)(2,1)} %collective-permute-done.19, bf16[1024,128]{1,0:T(8,128)(2,1)} %collective-permute-done.20, bf16[1024,128]{1,0:T(8,128)(2,1)} %collective-permute-done.21, bf16[3072,128]{1,0:T(8,128)(2,1)} %collective-permute-done.18, ...), kind=kLoop, calls=%fused_computation.15 | loop fusion | flops 3145728 | bytes 2883590 | tf_op jit(solution)/shard_map/convert_element_type | solution.py:347
  154.3 1.3 collective-permute-start.22
  156.5 1.6 add_bitcast_fusion
  158.1 7.9 %collective-permute-done.22 = bf16[1024,128]{1,0:T(8,128)(2,1)S(1)} collective-permute-done((bf16[1024,128]{1,0:T(8,128)(2,1)S(1)}, bf16[1024,128]{1,0:T(8,128)(2,1)S(1)}, u32[]{:S(2)}, u32[]{:S(2)}) %collective-permute-start.22) | collective-permute-done | bytes 262176 | tf_op jit(solution)/shard_map/ppermute | solution.py:327
  166.0 0.8 slice_add_fusion
  (92 shorter events, 9.2 us)
Async XLA Ops:
  7.2 9.7 %copy-start.14 = (s32[3]{0:T(128)S(1)}, s32[3]{0:T(128)}, u32[]{:S(2)}) copy-start(s32[3]{0:T(128)} %constant.82) | copy-start | bytes 40
  7.2 13.0 %copy-start.13 = (s32[4]{0:T(128)S(1)}, s32[4]{0:T(128)}, u32[]{:S(2)}) copy-start(s32[4]{0:T(128)} %constant.80) | copy-start | bytes 52
  7.2 66.5 %all-gather.2.cloned.1.call-start = ((), (), s32[]{:S(2)}) async-start(), calls=%async_computation.2 | async-start | bytes 4718592 | tf_op jit(solution)/shard_map/all_gather | solution.py:359
  7.9 29.6 %copy-start.12 = (s32[32,12]{0,1:T(8,128)S(1)}, s32[32,12]{0,1:T(8,128)}, u32[]{:S(2)}) copy-start(s32[32,12]{0,1:T(8,128)} %param.16) | copy-start | bytes 4612
  7.9 158.9 %reduce-scatter.2.cloned.1.call-start = ((), (), s32[]{:S(2)}) async-start(), calls=%async_computation.1 | async-start | bytes 4718592 | tf_op jit(solution)/shard_map/reduce_scatter | solution.py:402
  9.8 46.1 %copy-start.5 = (bf16[1024,128]{1,0:T(8,128)(2,1)}, bf16[1024,128]{1,0:T(8,128)(2,1)S(1)}, u32[]{:S(2)}) copy-start(bf16[1024,128]{1,0:T(8,128)(2,1)S(1)} %constant_dynamic-update-slice_fusion.refs_2_.refs_7_) | copy-start | bytes 786436
  9.8 8.9 %collective-permute-start.1 = (bf16[1024,128]{1,0:T(8,128)(2,1)S(1)}, bf16[1024,128]{1,0:T(8,128)(2,1)S(1)}, u32[]{:S(2)}, u32[]{:S(2)}) collective-permute-start(bf16[1024,128]{1,0:T(8,128)(2,1)S(1)} %constant_dynamic-update-slice_fusion.refs_2_.refs_7_), channel_id=1, source_target_pairs={{0,64},{8,72},{16,80},{24,88},{32,96},{40,104},{48,112},{56,120},{... | collective-permute-start | bytes 786440 | tf_op jit(solution)/shard_map/ppermute | solution.py:327
  15.8 29.6 %collective-permute-start = (bf16[1536,128]{1,0:T(8,128)(2,1)S(1)}, bf16[1536,128]{1,0:T(8,128)(2,1)S(1)}, u32[]{:S(2)}, u32[]{:S(2)}) collective-permute-start(bf16[1536,128]{1,0:T(8,128)(2,1)S(1)} %pad_maximum_fusion), channel_id=1, source_target_pairs={{0,8},{8,0},{16,24},{24,16},{32,40},{40,32},{48,56},{56,48},{64,72... | collective-permute-start | bytes 1179656 | tf_op jit(solution)/shard_map/ppermute | solution.py:327
  18.8 42.1 %copy-start.8 = (bf16[1024,128]{1,0:T(8,128)(2,1)}, bf16[1024,128]{1,0:T(8,128)(2,1)S(1)}, u32[]{:S(2)}) copy-start(bf16[1024,128]{1,0:T(8,128)(2,1)S(1)} %collective-permute-done.1.refs_5_.refs_8_) | copy-start | bytes 786436
  18.8 7.7 %collective-permute-start.2 = (bf16[1024,128]{1,0:T(8,128)(2,1)S(1)}, bf16[1024,128]{1,0:T(8,128)(2,1)S(1)}, u32[]{:S(2)}, u32[]{:S(2)}) collective-permute-start(bf16[1024,128]{1,0:T(8,128)(2,1)S(1)} %get-tuple-element.60), channel_id=1, source_target_pairs={{0,16},{8,24},{16,32},{24,40},{32,48},{40,56},{48,0},{56,8},{64,80... | collective-permute-start | bytes 786440 | tf_op jit(solution)/shard_map/ppermute | solution.py:327
  20.3 13.0 %collective-permute-start.3 = (bf16[1024,128]{1,0:T(8,128)(2,1)S(1)}, bf16[1024,128]{1,0:T(8,128)(2,1)S(1)}, u32[]{:S(2)}, u32[]{:S(2)}) collective-permute-start(bf16[1024,128]{1,0:T(8,128)(2,1)S(1)} %get-tuple-element.59), channel_id=1, source_target_pairs={{0,32},{8,40},{16,48},{24,56},{32,0},{40,8},{48,16},{56,24},{64,96... | collective-permute-start | bytes 786440 | tf_op jit(solution)/shard_map/ppermute | solution.py:327
  33.3 27.6 %copy-start.10 = (bf16[2048,128]{1,0:T(8,128)(2,1)}, bf16[2048,128]{1,0:T(8,128)(2,1)S(1)}, u32[]{:S(2)}) copy-start(bf16[2048,128]{1,0:T(8,128)(2,1)S(1)} %constant_dynamic-update-slice_fusion.2.refs_4_.refs_7_) | copy-start | bytes 1572868
  33.3 13.6 %collective-permute-start.8 = (bf16[2048,128]{1,0:T(8,128)(2,1)S(1)}, bf16[2048,128]{1,0:T(8,128)(2,1)S(1)}, u32[]{:S(2)}, u32[]{:S(2)}) collective-permute-start(bf16[2048,128]{1,0:T(8,128)(2,1)S(1)} %constant_dynamic-update-slice_fusion.2.refs_4_.refs_7_), channel_id=1, source_target_pairs={{0,64},{8,72},{16,80},{24,88},{32,96},{40,104},{48,112},{56,120},{... | collective-permute-start | bytes 1572872 | tf_op jit(solution)/shard_map/ppermute | solution.py:327
  37.8 7.7 %collective-permute-start.4 = (bf16[1024,128]{1,0:T(8,128)(2,1)S(1)}, bf16[1024,128]{1,0:T(8,128)(2,1)}, u32[]{:S(2)}, u32[]{:S(2)}) collective-permute-start(bf16[1024,128]{1,0:T(8,128)(2,1)S(1)} %get-tuple-element.58), channel_id=1, source_target_pairs={{0,48},{8,56},{16,0},{24,8},{32,16},{40,24},{48,32},{56,40},{64,11... | collective-permute-start | bytes 786440 | tf_op jit(solution)/shard_map/ppermute | solution.py:327
  37.9 14.5 %collective-permute-start.9 = (bf16[1024,128]{1,0:T(8,128)(2,1)S(1)}, bf16[1024,128]{1,0:T(8,128)(2,1)}, u32[]{:S(2)}, u32[]{:S(2)}) collective-permute-start(bf16[1024,128]{1,0:T(8,128)(2,1)S(1)} %collective-permute-done.1.refs_5_.refs_8_), channel_id=1, source_target_pairs={{0,64},{8,72},{16,80},{24,88},{32,96},{40,104},{48,112},{56,120},{... | collective-permute-start | bytes 786440 | tf_op jit(solution)/shard_map/ppermute | solution.py:327
  41.7 19.1 %collective-permute-start.5 = (bf16[2048,128]{1,0:T(8,128)(2,1)S(1)}, bf16[2048,128]{1,0:T(8,128)(2,1)S(1)}, u32[]{:S(2)}, u32[]{:S(2)}) collective-permute-start(bf16[2048,128]{1,0:T(8,128)(2,1)S(1)} %constant_dynamic-update-slice_fusion.2.refs_4_.refs_7_), channel_id=1, source_target_pairs={{0,8},{8,0},{16,24},{24,16},{32,40},{40,32},{48,56},{56,48},{64,72... | collective-permute-start | bytes 1572872 | tf_op jit(solution)/shard_map/ppermute | solution.py:327
  45.5 10.5 %copy-start.11 = (bf16[1536,128]{1,0:T(8,128)(2,1)}, bf16[1536,128]{1,0:T(8,128)(2,1)S(1)}, u32[]{:S(2)}) copy-start(bf16[1536,128]{1,0:T(8,128)(2,1)S(1)} %collective-permute-done.refs_3_.refs_8_) | copy-start | bytes 1179652
  45.5 15.4 %collective-permute-start.6 = (bf16[1024,128]{1,0:T(8,128)(2,1)S(1)}, bf16[1024,128]{1,0:T(8,128)(2,1)}, u32[]{:S(2)}, u32[]{:S(2)}) collective-permute-start(bf16[1024,128]{1,0:T(8,128)(2,1)S(1)} %collective-permute-done.1.refs_5_.refs_8_), channel_id=1, source_target_pairs={{0,8},{8,0},{16,24},{24,16},{32,40},{40,32},{48,56},{56,48},{64,72... | collective-permute-start | bytes 786440 | tf_op jit(solution)/shard_map/ppermute | solution.py:327
  45.5 15.4 %collective-permute-start.7 = (bf16[1024,128]{1,0:T(8,128)(2,1)}, bf16[1024,128]{1,0:T(8,128)(2,1)}, u32[]{:S(2)}, u32[]{:S(2)}) collective-permute-start(bf16[1024,128]{1,0:T(8,128)(2,1)} %collective-permute-done.4.refs_6_.refs_9_), channel_id=1, source_target_pairs={{0,8},{8,0},{16,24},{24,16},{32,40},{40,32},{48,56},{56,48},{64,72... | collective-permute-start | bytes 786440 | tf_op jit(solution)/shard_map/ppermute | solution.py:327
  46.9 17.0 %copy-start.15 = (bf16[2048,128]{1,0:T(8,128)(2,1)}, bf16[2048,128]{1,0:T(8,128)(2,1)S(1)}, u32[]{:S(2)}) copy-start(bf16[2048,128]{1,0:T(8,128)(2,1)S(1)} %collective-permute-done.8.refs_4_.refs_7_) | copy-start | bytes 1572868
  46.9 17.0 %collective-permute-start.10 = (bf16[2048,128]{1,0:T(8,128)(2,1)S(1)}, bf16[2048,128]{1,0:T(8,128)(2,1)S(1)}, u32[]{:S(2)}, u32[]{:S(2)}) collective-permute-start(bf16[2048,128]{1,0:T(8,128)(2,1)S(1)} %collective-permute-done.8.refs_4_.refs_7_), channel_id=1, source_target_pairs={{0,8},{8,0},{16,24},{24,16},{32,40},{40,32},{48,56},{56,48},{64,72... | collective-permute-start | bytes 1572872 | tf_op jit(solution)/shard_map/ppermute | solution.py:327
  52.4 11.5 %collective-permute-start.11 = (bf16[1024,128]{1,0:T(8,128)(2,1)}, bf16[1024,128]{1,0:T(8,128)(2,1)}, u32[]{:S(2)}, u32[]{:S(2)}) collective-permute-start(bf16[1024,128]{1,0:T(8,128)(2,1)} %collective-permute-done.9.refs_5_.refs_8_), channel_id=1, source_target_pairs={{0,8},{8,0},{16,24},{24,16},{32,40},{40,32},{48,56},{56,48},{64,72... | collective-permute-start | bytes 786440 | tf_op jit(solution)/shard_map/ppermute | solution.py:327
  60.9 0.8 copy-start.16
  63.9 0.8 copy-start.17
  64.7 5.0 %copy-start = (bf16[256,4096]{1,0:T(8,128)(2,1)S(1)}, bf16[256,4096]{1,0:T(8,128)(2,1)}, u32[]{:S(2)}) copy-start(bf16[256,4096]{1,0:T(8,128)(2,1)} %refs_7_.1) | copy-start | bytes 6291460
  67.0 1.6 collective-permute-start.12
  69.7 3.3 %copy-start.1 = (bf16[512,256]{1,0:T(8,128)(2,1)}, bf16[512,256]{1,0:T(8,128)(2,1)S(1)}, u32[]{:S(2)}) copy-start(bf16[512,256]{1,0:T(8,128)(2,1)S(1)} %maximum_select_fusion.1.a_ref) | copy-start | bytes 786436
  81.2 11.9 %collective-permute-start.23 = (bf16[16,256,128]{2,1,0:T(8,128)(2,1)}, bf16[16,256,128]{2,1,0:T(8,128)(2,1)S(1)}, u32[]{:S(2)}, u32[]{:S(2)}) collective-permute-start(bf16[16,256,128]{2,1,0:T(8,128)(2,1)} %get-tuple-element.50), channel_id=1, source_target_pairs={{0,8},{8,0},{16,24},{24,16},{32,40},{40,32},{48,56},{56,48},{64,72... | collective-permute-start | bytes 3145736 | tf_op jit(solution)/shard_map/ppermute | solution.py:327
  81.4 2.9 %collective-permute-start.13 = (bf16[512,128]{1,0:T(8,128)(2,1)}, bf16[512,128]{1,0:T(8,128)(2,1)S(1)}, u32[]{:S(2)}, u32[]{:S(2)}) collective-permute-start(bf16[512,128]{1,0:T(8,128)(2,1)} %get-tuple-element.35), channel_id=1, source_target_pairs={{0,8},{8,0},{16,24},{24,16},{32,40},{40,32},{48,56},{56,48},{64,72... | collective-permute-start | bytes 393224 | tf_op jit(solution)/shard_map/ppermute | solution.py:327
  88.5 6.8 %collective-permute-start.17 = (bf16[3072,128]{1,0:T(8,128)(2,1)}, bf16[3072,128]{1,0:T(8,128)(2,1)S(1)}, u32[]{:S(2)}, u32[]{:S(2)}) collective-permute-start(bf16[3072,128]{1,0:T(8,128)(2,1)} %get-tuple-element.48), channel_id=1, source_target_pairs={{0,8},{8,0},{16,24},{24,16},{32,40},{40,32},{48,56},{56,48},{64,72... | collective-permute-start | bytes 2359304 | tf_op jit(solution)/shard_map/ppermute | solution.py:327
  88.7 4.3 %copy-start.2 = (bf16[16,256,128]{2,1,0:T(8,128)(2,1)S(1)}, bf16[16,256,128]{2,1,0:T(8,128)(2,1)}, u32[]{:S(2)}) copy-start(bf16[16,256,128]{2,1,0:T(8,128)(2,1)} %get-tuple-element.49) | copy-start | bytes 3145732
  92.6 2.7 %copy-start.4 = (bf16[3072,128]{1,0:T(8,128)(2,1)S(1)}, bf16[3072,128]{1,0:T(8,128)(2,1)}, u32[]{:S(2)}) copy-start(bf16[3072,128]{1,0:T(8,128)(2,1)} %get-tuple-element.47) | copy-start | bytes 2359300
  92.6 41.8 %collective-permute-start.16 = (bf16[4096,128]{1,0:T(8,128)(2,1)}, bf16[4096,128]{1,0:T(8,128)(2,1)}, u32[]{:S(2)}, u32[]{:S(2)}) collective-permute-start(bf16[4096,128]{1,0:T(8,128)(2,1)} %get-tuple-element.46), channel_id=1, source_target_pairs={{0,8},{8,0},{16,24},{24,16},{32,40},{40,32},{48,56},{56,48},{64,72... | collective-permute-start | bytes 3145736 | tf_op jit(solution)/shard_map/ppermute | solution.py:327
  93.2 14.4 %collective-permute-start.24 = (bf16[8,256,128]{2,1,0:T(8,128)(2,1)S(1)}, bf16[8,256,128]{2,1,0:T(8,128)(2,1)S(1)}, u32[]{:S(2)}, u32[]{:S(2)}) collective-permute-start(bf16[8,256,128]{2,1,0:T(8,128)(2,1)S(1)} %add_convert_fusion.1), channel_id=1, source_target_pairs={{0,16},{8,24},{16,0},{24,8},{32,48},{40,56},{48,32},{56,40},{64,80... | collective-permute-start | bytes 1572872 | tf_op jit(solution)/shard_map/ppermute | solution.py:327
  96.5 38.0 %collective-permute-start.18 = (bf16[3072,128]{1,0:T(8,128)(2,1)}, bf16[3072,128]{1,0:T(8,128)(2,1)}, u32[]{:S(2)}, u32[]{:S(2)}) collective-permute-start(bf16[3072,128]{1,0:T(8,128)(2,1)} %add_convert_fusion), channel_id=1, source_target_pairs={{64,0},{72,8},{80,16},{88,24},{96,32},{104,40},{112,48},{120,56},{... | collective-permute-start | bytes 2359304 | tf_op jit(solution)/shard_map/ppermute | solution.py:327
  107.6 9.7 %copy-start.6 = (bf16[8,256,128]{2,1,0:T(8,128)(2,1)}, bf16[8,256,128]{2,1,0:T(8,128)(2,1)S(1)}, u32[]{:S(2)}) copy-start(bf16[8,256,128]{2,1,0:T(8,128)(2,1)S(1)} %collective-permute-done.24) | copy-start | bytes 1572868
  108.5 16.9 %collective-permute-start.25 = (bf16[4,256,128]{2,1,0:T(8,128)(2,1)}, bf16[4,256,128]{2,1,0:T(8,128)(2,1)}, u32[]{:S(2)}, u32[]{:S(2)}) collective-permute-start(bf16[4,256,128]{2,1,0:T(8,128)(2,1)} %add_convert_fusion.2), channel_id=1, source_target_pairs={{0,32},{8,40},{16,48},{24,56},{32,0},{40,8},{48,16},{56,24},{64,96... | collective-permute-start | bytes 786440 | tf_op jit(solution)/shard_map/ppermute | solution.py:327
  117.3 17.1 %copy-start.3 = (bf16[4096,128]{1,0:T(8,128)(2,1)S(1)}, bf16[4096,128]{1,0:T(8,128)(2,1)}, u32[]{:S(2)}) copy-start(bf16[4096,128]{1,0:T(8,128)(2,1)} %get-tuple-element.45) | copy-start | bytes 3145732
  124.1 28.4 %copy-start.7 = (bf16[1024,128]{1,0:T(8,128)(2,1)S(1)}, bf16[1024,128]{1,0:T(8,128)(2,1)}, u32[]{:S(2)}) copy-start(bf16[1024,128]{1,0:T(8,128)(2,1)} %get-tuple-element.43) | copy-start | bytes 786436
  124.2 18.6 %collective-permute-start.15 = (bf16[1024,128]{1,0:T(8,128)(2,1)}, bf16[1024,128]{1,0:T(8,128)(2,1)}, u32[]{:S(2)}, u32[]{:S(2)}) collective-permute-start(bf16[1024,128]{1,0:T(8,128)(2,1)} %get-tuple-element.44), channel_id=1, source_target_pairs={{0,8},{8,0},{16,24},{24,16},{32,40},{40,32},{48,56},{56,48},{64,72... | collective-permute-start | bytes 786440 | tf_op jit(solution)/shard_map/ppermute | solution.py:327
  126.5 12.1 %collective-permute-start.26 = (bf16[2,256,128]{2,1,0:T(8,128)(2,1)S(1)}, bf16[2,256,128]{2,1,0:T(8,128)(2,1)}, u32[]{:S(2)}, u32[]{:S(2)}) collective-permute-start(bf16[2,256,128]{2,1,0:T(8,128)(2,1)S(1)} %add_convert_fusion.6), channel_id=1, source_target_pairs={{0,64},{8,72},{16,80},{24,88},{32,96},{40,104},{48,112},{56,120},{... | collective-permute-start | bytes 393224 | tf_op jit(solution)/shard_map/ppermute | solution.py:327
  136.8 11.7 %collective-permute-start.19 = (bf16[1024,128]{1,0:T(8,128)(2,1)}, bf16[1024,128]{1,0:T(8,128)(2,1)}, u32[]{:S(2)}, u32[]{:S(2)}) collective-permute-start(bf16[1024,128]{1,0:T(8,128)(2,1)} %get-tuple-element.52), channel_id=1, source_target_pairs={{0,48},{8,56},{16,0},{24,8},{32,16},{40,24},{48,32},{56,40},{64,11... | collective-permute-start | bytes 786440 | tf_op jit(solution)/shard_map/ppermute | solution.py:327
  137.1 11.4 %collective-permute-start.20 = (bf16[1024,128]{1,0:T(8,128)(2,1)}, bf16[1024,128]{1,0:T(8,128)(2,1)}, u32[]{:S(2)}, u32[]{:S(2)}) collective-permute-start(bf16[1024,128]{1,0:T(8,128)(2,1)} %get-tuple-element.51), channel_id=1, source_target_pairs={{0,32},{8,40},{16,48},{24,56},{32,0},{40,8},{48,16},{56,24},{64,96... | collective-permute-start | bytes 786440 | tf_op jit(solution)/shard_map/ppermute | solution.py:327
  138.0 14.6 %collective-permute-start.21 = (bf16[1024,128]{1,0:T(8,128)(2,1)}, bf16[1024,128]{1,0:T(8,128)(2,1)}, u32[]{:S(2)}, u32[]{:S(2)}) collective-permute-start(bf16[1024,128]{1,0:T(8,128)(2,1)} %get-tuple-element.53), channel_id=1, source_target_pairs={{0,16},{8,24},{16,32},{24,40},{32,48},{40,56},{48,0},{56,8},{64,80... | collective-permute-start | bytes 786440 | tf_op jit(solution)/shard_map/ppermute | solution.py:327
  138.6 17.0 %copy-start.9 = (f32[512,128]{1,0:T(8,128)S(1)}, f32[512,128]{1,0:T(8,128)}, u32[]{:S(2)}) copy-start(f32[512,128]{1,0:T(8,128)} %get-tuple-element.41) | copy-start | bytes 786436
  138.6 17.0 %collective-permute-start.14 = (f32[512,128]{1,0:T(8,128)}, f32[512,128]{1,0:T(8,128)S(1)}, u32[]{:S(2)}, u32[]{:S(2)}) collective-permute-start(f32[512,128]{1,0:T(8,128)} %get-tuple-element.42), channel_id=1, source_target_pairs={{0,8},{8,0},{16,24},{24,16},{32,40},{40,32},{48,56},{56,48},{64,72... | collective-permute-start | bytes 786440 | tf_op jit(solution)/shard_map/ppermute | solution.py:327
  142.8 13.7 %collective-permute-start.27 = (bf16[1,256,128]{2,1,0:T(8,128)(2,1)S(1)}, bf16[1,256,128]{2,1,0:T(8,128)(2,1)S(1)}, u32[]{:S(2)}, u32[]{:S(2)}) collective-permute-start(bf16[1,256,128]{2,1,0:T(8,128)(2,1)S(1)} %add_convert_fusion.7), channel_id=1, source_target_pairs={{0,128},{8,136},{16,144},{24,152},{32,160},{40,168},{48,176},{56,1... | collective-permute-start | bytes 196616 | tf_op jit(solution)/shard_map/ppermute | solution.py:327
  154.3 11.7 %collective-permute-start.22 = (bf16[1024,128]{1,0:T(8,128)(2,1)S(1)}, bf16[1024,128]{1,0:T(8,128)(2,1)S(1)}, u32[]{:S(2)}, u32[]{:S(2)}) collective-permute-start(bf16[1024,128]{1,0:T(8,128)(2,1)S(1)} %get-tuple-element.56), channel_id=1, source_target_pairs={{64,0},{72,8},{80,16},{88,24},{96,32},{104,40},{112,48},{120,56},{... | collective-permute-start | bytes 786440 | tf_op jit(solution)/shard_map/ppermute | solution.py:327
  (1 other events, 0.7 us)
Sparse Core Ops, SparseCore 0:
  9.8 58.3 all-gather.1
  73.2 65.9 reduce-scatter.1

commit v2 on v1

--- a/solution.py
+++ b/solution.py
@@ -258,13 +258,6 @@
     )(flags, q2, do_own, do_sib, lse, *state, *arrays)
 
 
-ORDER = (0, 2, 1, 3)
-
-
-def order(i):
-    return (i % 2) * 2 + i // 2
-
-
 def grads_body(where_ref, a_ref, *refs):
     pieces, weights = refs[:4], refs[4:8]
     keep_ref, give_ref, mine_ref, other_ref, at, acc = refs[8:]
@@ -296,7 +289,7 @@
     rows, width = attn.shape
 
     def column(i):
-        return lambda p, w: (0, 4 * (w[0] ^ ORDER[i]) + (w[1] ^ order(p)))
+        return lambda p, w: (0, 4 * (w[0] ^ (p % 2 + i // 2 * 2)) + (w[1] ^ (p // 2 + i % 2 * 2)))
 
     out = jax.ShapeDtypeStruct((16, width, 128), BF16)
     spec = pl.BlockSpec((4, width, 128), lambda p, w: (p, 0, 0))
@@ -383,7 +376,7 @@
     farx = swap(far)
     q2 = jnp.stack([mine_of(query_proj), ownx[KV:]])
 
-    keys = jnp.concatenate([b - 2 * jnp.array(d) for d in ([0], [1, 2, 4, 3], [5, 6, 8]) for b in (rank, sib)])
+    keys = jnp.concatenate([b - 2 * jnp.array(d) for d in ([0], [1, 2, 4, 3], [5, 6, 8], [0, 1, 2, 4, 3]) for b in (rank, sib)])
     lists = jnp.stack(
         [lax.dynamic_index_in_dim(attended_blocks, r, 0, keepdims=False) for r in (rank, sib)]
     )
@@ -392,6 +385,7 @@
     self_blocks = ([own, ownx], ((0, 0), (1, 0)))
     near_blocks = ([pre, x1, d3, prex, x1x, d3x], ((0, 0), (0, KV), (1, 0), (2, 0), (3, 0), (3, KV), (4, 0), (5, 0)))
     far_blocks = ([far, d8, farx, d8x], ((0, 0), (0, KV), (1, 0), (2, 0), (2, KV), (3, 0)))
+    all_blocks = ([own, ownx] + near_blocks[0], ((0, 0), (2, 0), (2, KV), (3, 0), (4, 0), (1, 0), (5, 0), (5, KV), (6, 0), (7, 0)))
     state = fwd_call(flags, 0, q2, None, *self_blocks, diag=1)
     state = fwd_call(flags, 2, q2, state, *near_blocks)
     attn_own, attn_sib, lse = fwd_call(flags, 10, q2, state, *far_blocks, last=True)
@@ -414,30 +408,29 @@
     came = back(bf(f32(keep) + f32(got)))
     parts, gave = summed(8, [wkeep], wcame)
     wcame = send(gave, lambda x, y, c: (x, y ^ 1, c))
-    dq, delta, keep, give = bwd_call(flags, 2, *args, (dq, delta), *near_blocks)
+    dq_own, dq_sib, keep, give = bwd_call(flags, 16, *args, (dq, delta), *all_blocks, diag=5, last=True)
     got = swap(give)
-    dq_own, dq_sib, keep0, give0 = bwd_call(flags, 0, *args, (dq, delta), *self_blocks, diag=1, last=True)
-    got0 = swap(give0)
     dq_other = swap(dq_sib)
     parts, gave = summed(4, parts, wcame)
-    wcame = send(gave, lambda x, y, c: (x, y ^ 2, c))
-    t1, t2, t4 = [f32(keep[at]) + f32(got[at]) + f32(came[at]) for at in (slice(i, i + KV) for i in (0, KV, 2 * KV))]
-    t3 = f32(keep[3 * KV :]) + f32(got[3 * KV :])
+    wcame = send(gave, lambda x, y, c: (x ^ 1, y, c))
+    t0, t1, t2, t4, t3 = [f32(keep[at]) + f32(got[at]) for at in (slice(i * KV, (i + 1) * KV) for i in range(5))]
+    t1, t2, t4 = [t + f32(came[i * KV : (i + 1) * KV]) for i, t in enumerate((t1, t2, t4))]
     s1 = along(bf(t1), -1)
     s2 = along(bf(t2), -2)
     s3 = along(bf(t3), -3)
     parts, gave = summed(2, parts, wcame)
-    wcame = send(gave, lambda x, y, c: (x ^ 1, y, c))
+    wcame = send(gave, lambda x, y, c: (x ^ 2, y, c))
 
     def kept(cond, v):
         return jnp.where(cond, f32(v), 0.0)
 
     r4 = back(bf(t4 + kept(y == 3, s1) + kept(y >= 2, s2) + kept(y >= 1, s3)))
     parts, gave = summed(1, parts, wcame)
-    wcame = send(gave, lambda x, y, c: (x ^ 2, y, c))
-    grad_wout = sum(f32(p[0]) for p in parts) + f32(wcame[0])
+    gave, part = lax.optimization_barrier((gave, sum(f32(p[0]) for p in parts)))
+    wcame = send(gave, lambda x, y, c: (x, y ^ 2, c))
+    grad_wout = part + f32(wcame[0])
     grad_query = joined(dq_own, dq_other)
-    total = f32(keep0) + f32(got0) + kept(y < 3, s1) + kept(y < 2, s2) + kept(y < 1, s3)
+    total = t0 + kept(y < 3, s1) + kept(y < 2, s2) + kept(y < 1, s3)
     total = lax.optimization_barrier(total)
     grad_key, grad_value = [total[at] + f32(r4[at]) for at in (slice(0, BT), slice(BT, KV))]
     return (layer_out, grad_query, grad_key, grad_value, grad_wout)

time: 176 us -> 185 us (1.051)
  waiting for transfers between devices: 38.9 us -> 55.2 us
  Pallas kernels: 31.1 us -> 28.2 us
  other arithmetic: 16.3 us -> 13.9 us
    ppermute x28 -> x27, waiting for transfers between devices: 38.2 us -> 54.5 us  [send(): return lax.ppermute(value, 'ctx', pairs)]
    pallas_call x3 -> x2, Pallas kernels: 14.2 us -> 11.2 us  [bwd_call(): pl.pallas_call(functools.partial(bwd_body, base, plan, diag, first, last)...]
    convert_element_type x7 -> x6, other arithmetic: 8.3 us -> 6.63 us  [bf(): return v.astype(BF16)]
    ppermute x28 -> x27, starting transfers between devices: 64.4 us -> 63.7 us  [send(): return lax.ppermute(value, 'ctx', pairs)]
  transfers between devices with their start and end apart: 30 -> 29, of which waited for: 8 -> 10; matrix products, arithmetic and copies ran while one was open for 13% -> 11% of each run, Pallas kernels for 18% -> 15%
where the time goes in v2:
time: 185 us; the launch traced here: 184 us
  starting transfers between devices  63.7 us (34%)
  waiting for transfers between devices  55.2 us (30%)
  Pallas kernels  28.2 us (15%)
  between operations  14.5 us (8%)
  other arithmetic  13.9 us (8%)
  local copies, waits for them, and re-layouts  5.22 us (3%)
  matrix products  3.26 us (2%)
    ppermute x27, starting transfers between devices, send(): return lax.ppermute(value, 'ctx', pairs)  63.7 us
    ppermute x27, waiting for transfers between devices, send(): return lax.ppermute(value, 'ctx', pairs)  54.5 us
    pallas_call x2, Pallas kernels, bwd_call(): pl.pallas_call(functools.partial(bwd_body, base, plan, diag, first, last)...  11.2 us
    pallas_call x3, Pallas kernels, fwd_call(): pl.pallas_call(functools.partial(fwd_body, base, plan, diag, first, last)...  9.44 us
    pallas_call x1, Pallas kernels, grads_call(): pl.pallas_call(grads_body, grid_spec=pltpu.PrefetchScalarGridSpec(num_sca...  7.56 us
    convert_element_type x6, other arithmetic, bf(): return v.astype(BF16)  6.63 us
  transfers between devices with their start and end apart: 29, of which 10 were waited for; matrix products, arithmetic and copies ran while one was open for 11% of the time, Pallas kernels for 15%

profile of v2, /device:TPU:1, one launch (start us, length us, event | category | flops | bytes accessed | tf_op | source)
XLA Modules:
  0.0 184.0 jit_solution(12951232409979020103)
XLA Ops:
  8.0 0.9 constant_dynamic-update-slice_fusion.1
  8.9 0.9 constant_dynamic-update-slice_fusion.refs_2_.refs_7_
  9.9 3.9 %collective-permute-start.1 = (bf16[1024,128]{1,0:T(8,128)(2,1)S(1)}, bf16[1024,128]{1,0:T(8,128)(2,1)S(1)}, u32[]{:S(2)}, u32[]{:S(2)}) collective-permute-start(bf16[1024,128]{1,0:T(8,128)(2,1)S(1)} %constant_dynamic-update-slice_fusion.refs_2_.refs_7_), channel_id=1, source_target_pairs={{0,64},{8,72},{16,80},{24,88},{32,96},{40,104},{48,112},{56,120},{... | collective-permute-start | bytes 786440 | tf_op jit(solution)/shard_map/ppermute | solution.py:320
  13.8 1.0 select_bitcast_fusion
  14.9 1.0 collective-permute-start
  16.0 2.8 %collective-permute-done.1.refs_5_.refs_10_ = bf16[1024,128]{1,0:T(8,128)(2,1)S(1)} collective-permute-done((bf16[1024,128]{1,0:T(8,128)(2,1)S(1)}, bf16[1024,128]{1,0:T(8,128)(2,1)S(1)}, u32[]{:S(2)}, u32[]{:S(2)}) %collective-permute-start.1) | collective-permute-done | bytes 262176 | tf_op jit(solution)/shard_map/ppermute | solution.py:320
  18.8 1.4 collective-permute-start.2
  20.3 2.7 %collective-permute-start.3 = (bf16[1024,128]{1,0:T(8,128)(2,1)S(1)}, bf16[1024,128]{1,0:T(8,128)(2,1)S(1)}, u32[]{:S(2)}, u32[]{:S(2)}) collective-permute-start(bf16[1024,128]{1,0:T(8,128)(2,1)S(1)} %get-tuple-element.57), channel_id=1, source_target_pairs={{0,32},{8,40},{16,48},{24,56},{32,0},{40,8},{48,16},{56,24},{64,96... | collective-permute-start | bytes 786440 | tf_op jit(solution)/shard_map/ppermute | solution.py:320
  23.0 3.6 %collective-permute-done.2 = bf16[1024,128]{1,0:T(8,128)(2,1)S(1)} collective-permute-done((bf16[1024,128]{1,0:T(8,128)(2,1)S(1)}, bf16[1024,128]{1,0:T(8,128)(2,1)S(1)}, u32[]{:S(2)}, u32[]{:S(2)}) %collective-permute-start.2) | collective-permute-done | bytes 262176 | tf_op jit(solution)/shard_map/ppermute | solution.py:320
  26.6 6.7 %collective-permute-done.3 = bf16[1024,128]{1,0:T(8,128)(2,1)S(1)} collective-permute-done((bf16[1024,128]{1,0:T(8,128)(2,1)S(1)}, bf16[1024,128]{1,0:T(8,128)(2,1)S(1)}, u32[]{:S(2)}, u32[]{:S(2)}) %collective-permute-start.3) | collective-permute-done | bytes 262176 | tf_op jit(solution)/shard_map/ppermute | solution.py:320
  33.4 4.1 %collective-permute-start.8 = (bf16[2048,128]{1,0:T(8,128)(2,1)S(1)}, bf16[2048,128]{1,0:T(8,128)(2,1)S(1)}, u32[]{:S(2)}, u32[]{:S(2)}) collective-permute-start(bf16[2048,128]{1,0:T(8,128)(2,1)S(1)} %constant_dynamic-update-slice_fusion.2.refs_4_.refs_9_), channel_id=1, source_target_pairs={{0,64},{8,72},{16,80},{24,88},{32,96},{40,104},{48,112},{56,120},{... | collective-permute-start | bytes 1572872 | tf_op jit(solution)/shard_map/ppermute | solution.py:320
  37.9 3.1 %collective-permute-start.9 = (bf16[1024,128]{1,0:T(8,128)(2,1)S(1)}, bf16[1024,128]{1,0:T(8,128)(2,1)S(1)}, u32[]{:S(2)}, u32[]{:S(2)}) collective-permute-start(bf16[1024,128]{1,0:T(8,128)(2,1)S(1)} %collective-permute-done.1.refs_5_.refs_10_), channel_id=1, source_target_pairs={{0,64},{8,72},{16,80},{24,88},{32,96},{40,104},{48,112},{56,120},{... | collective-permute-start | bytes 786440 | tf_op jit(solution)/shard_map/ppermute | solution.py:320
  41.0 3.0 %collective-permute-start.5 = (bf16[2048,128]{1,0:T(8,128)(2,1)S(1)}, bf16[2048,128]{1,0:T(8,128)(2,1)}, u32[]{:S(2)}, u32[]{:S(2)}) collective-permute-start(bf16[2048,128]{1,0:T(8,128)(2,1)S(1)} %constant_dynamic-update-slice_fusion.2.refs_4_.refs_9_), channel_id=1, source_target_pairs={{0,8},{8,0},{16,24},{24,16},{32,40},{40,32},{48,56},{56,48},{64,72... | collective-permute-start | bytes 1572872 | tf_op jit(solution)/shard_map/ppermute | solution.py:320
  44.8 2.0 %collective-permute-start.7 = (bf16[1024,128]{1,0:T(8,128)(2,1)S(1)}, bf16[1024,128]{1,0:T(8,128)(2,1)S(1)}, u32[]{:S(2)}, u32[]{:S(2)}) collective-permute-start(bf16[1024,128]{1,0:T(8,128)(2,1)S(1)} %collective-permute-done.4.refs_6_.refs_11_), channel_id=1, source_target_pairs={{0,8},{8,0},{16,24},{24,16},{32,40},{40,32},{48,56},{56,48},{64,72... | collective-permute-start | bytes 786440 | tf_op jit(solution)/shard_map/ppermute | solution.py:320
  46.8 5.6 %collective-permute-start.10 = (bf16[2048,128]{1,0:T(8,128)(2,1)S(1)}, bf16[2048,128]{1,0:T(8,128)(2,1)S(1)}, u32[]{:S(2)}, u32[]{:S(2)}) collective-permute-start(bf16[2048,128]{1,0:T(8,128)(2,1)S(1)} %collective-permute-done.8.refs_4_.refs_7_), channel_id=1, source_target_pairs={{0,8},{8,0},{16,24},{24,16},{32,40},{40,32},{48,56},{56,48},{64,72... | collective-permute-start | bytes 1572872 | tf_op jit(solution)/shard_map/ppermute | solution.py:320
  52.5 2.7 %collective-permute-start.11 = (bf16[1024,128]{1,0:T(8,128)(2,1)S(1)}, bf16[1024,128]{1,0:T(8,128)(2,1)}, u32[]{:S(2)}, u32[]{:S(2)}) collective-permute-start(bf16[1024,128]{1,0:T(8,128)(2,1)S(1)} %collective-permute-done.9.refs_5_.refs_8_), channel_id=1, source_target_pairs={{0,8},{8,0},{16,24},{24,16},{32,40},{40,32},{48,56},{56,48},{64,72... | collective-permute-start | bytes 786440 | tf_op jit(solution)/shard_map/ppermute | solution.py:320
  56.0 4.9 %fwd.3 = (f32[2,2,512]{2,1,0:T(2,128)}, f32[2,128,512]{2,1,0:T(8,128)}) custom-call(s32[52]{0:T(128)} %reshape.86.refs_0_, bf16[2,512,128]{2,1,0:T(8,128)(2,1)} %pad_maximum_fusion.1.refs_1_, bf16[1024,128]{1,0:T(8,128)(2,1)} %copy-done.6, bf16[1536,128]{1,0:T(8,128)(2,1)} %copy-done.14), custom_call_target="tpu_custom_call" | custom-call | flops 536870912 | bytes 524288 | tf_op jit(solution)/shard_map/fwd/pallas_call | solution.py:128
  61.7 2.3 %fwd.4 = (f32[2,2,512]{2,1,0:T(2,128)}, f32[2,128,512]{2,1,0:T(8,128)}) custom-call(s32[52]{0:T(128)} %reshape.86.refs_0_, bf16[2,512,128]{2,1,0:T(8,128)(2,1)} %pad_maximum_fusion.1.refs_1_, f32[2,2,512]{2,1,0:T(2,128)} %get-tuple-element.26.refs_2_, f32[2,128,512]{2,1,0:T(8,128)} %get-tuple-element.27.refs_3_, bf16[2048,128]{1,0:T(8,128)(2,1)} %copy-done.13, ...), custom_call_target="tpu_custom_call" | custom-call | flops 2147483648 | bytes 2097152 | tf_op jit(solution)/shard_map/fwd/pallas_call | solution.py:128
  64.8 2.3 %fwd.5 = (bf16[512,128]{1,0:T(8,128)(2,1)}, bf16[512,128]{1,0:T(8,128)(2,1)}, f32[2,512]{1,0:T(2,128)}) custom-call(s32[52]{0:T(128)} %reshape.86.refs_0_, bf16[2,512,128]{2,1,0:T(8,128)(2,1)} %pad_maximum_fusion.1.refs_1_, f32[2,2,512]{2,1,0:T(2,128)} %get-tuple-element.28.refs_2_, f32[2,128,512]{2,1,0:T(8,128)} %get-tuple-element.29.refs_3_, ...), custom_call_target="tpu_custom_call" | custom-call | flops 1610612736 | bytes 1572864 | tf_op jit(solution)/shard_map/fwd/pallas_call | solution.py:128
  67.2 1.5 collective-permute-done.12
  68.7 1.1 maximum_select_fusion.1.a_ref
  69.8 3.3 %convolution_convert_fusion = bf16[512,4096]{1,0:T(8,128)(2,1)} fusion(bf16[512,256]{1,0:T(8,128)(2,1)S(1)} %maximum_select_fusion.1.a_ref, bf16[256,4096]{1,0:T(8,128)(2,1)S(1)} %copy-done), kind=kOutput, calls=%fused_computation | convolution fusion | flops 1075838976 | bytes 6553600 | tf_op jit(solution)/shard_map/dot_general | solution.py:395
  73.8 7.6 %grads.1 = (bf16[16,256,128]{2,1,0:T(8,128)(2,1)}, bf16[16,256,128]{2,1,0:T(8,128)(2,1)}, bf16[512,128]{1,0:T(8,128)(2,1)}, bf16[512,128]{1,0:T(8,128)(2,1)}) custom-call(s32[3]{0:T(128)} %pad_add_fusion.1.where_ref, bf16[512,256]{1,0:T(8,128)(2,1)} %copy-done.1, bf16[512,4096]{1,0:T(8,128)(2,1)} %all-gather.2.cloned.1.call-done.refs_0_.refs_1_.refs_2_.refs_3_, ...), custom_call_target="tpu_custom_call" | custom-call | flops 2147483648 | bytes 8912896 | tf_op jit(solution)/shard_map/grads/pallas_call | solution.py:296
  81.9 1.0 collective-permute-done.13.refs_3_
  83.7 3.5 %bwd.2 = (f32[2,128,512]{2,1,0:T(8,128)}, f32[2,512]{1,0:T(2,128)}, bf16[3072,128]{1,0:T(8,128)(2,1)}, bf16[3072,128]{1,0:T(8,128)(2,1)}) custom-call(s32[52]{0:T(128)} %reshape.86.refs_0_, bf16[2,512,128]{2,1,0:T(8,128)(2,1)} %pad_maximum_fusion.1.refs_1_, bf16[512,128]{1,0:T(8,128)(2,1)} %get-tuple-element.32.refs_2_, bf16[512,128]{1,0:T(8,128)(2,1)} %copy-done.25, ...), custom_call_target="tpu_custom_call" | custom-call | flops 4026531840 | bytes 3145728 | tf_op jit(solution)/shard_map/bwd/pallas_call | solution.py:241
  87.4 7.7 %bwd.3 = (f32[512,128]{1,0:T(8,128)}, f32[512,128]{1,0:T(8,128)}, bf16[5120,128]{1,0:T(8,128)(2,1)}, bf16[5120,128]{1,0:T(8,128)(2,1)}) custom-call(s32[52]{0:T(128)} %reshape.86.refs_0_, bf16[2,512,128]{2,1,0:T(8,128)(2,1)} %pad_maximum_fusion.1.refs_1_, bf16[512,128]{1,0:T(8,128)(2,1)} %get-tuple-element.32.refs_2_, bf16[512,128]{1,0:T(8,128)(2,1)} %copy-done.25, ...), custom_call_target="tpu_custom_call" | custom-call | flops 6710886400 | bytes 5242880 | tf_op jit(solution)/shard_map/bwd/pallas_call | solution.py:241
  95.8 1.2 collective-permute-start.23
  97.0 1.4 add_convert_fusion
  98.4 1.3 collective-permute-start.17
  99.7 9.5 %collective-permute-done.23 = bf16[8,256,128]{2,1,0:T(8,128)(2,1)S(1)} collective-permute-done((bf16[8,256,128]{2,1,0:T(8,128)(2,1)S(1)}, bf16[8,256,128]{2,1,0:T(8,128)(2,1)S(1)}, u32[]{:S(2)}, u32[]{:S(2)}) %collective-permute-start.23) | collective-permute-done | bytes 524320 | tf_op jit(solution)/shard_map/ppermute | solution.py:320
  109.3 1.3 add_convert_fusion.2
  110.6 11.9 %collective-permute-start.24 = (bf16[4,256,128]{2,1,0:T(8,128)(2,1)S(1)}, bf16[4,256,128]{2,1,0:T(8,128)(2,1)S(1)}, u32[]{:S(2)}, u32[]{:S(2)}) collective-permute-start(bf16[4,256,128]{2,1,0:T(8,128)(2,1)S(1)} %add_convert_fusion.2), channel_id=1, source_target_pairs={{0,64},{8,72},{16,80},{24,88},{32,96},{40,104},{48,112},{56,120},{... | collective-permute-start | bytes 786440 | tf_op jit(solution)/shard_map/ppermute | solution.py:320
  122.5 12.8 %collective-permute-done.24 = bf16[4,256,128]{2,1,0:T(8,128)(2,1)S(1)} collective-permute-done((bf16[4,256,128]{2,1,0:T(8,128)(2,1)S(1)}, bf16[4,256,128]{2,1,0:T(8,128)(2,1)S(1)}, u32[]{:S(2)}, u32[]{:S(2)}) %collective-permute-start.24) | collective-permute-done | bytes 262176 | tf_op jit(solution)/shard_map/ppermute | solution.py:320
  135.3 1.1 add_convert_fusion.6
  136.5 1.8 collective-permute-start.25
  138.3 1.1 add_convert_fusion.4
  139.3 9.9 %collective-permute-start.18 = (bf16[1024,128]{1,0:T(8,128)(2,1)}, bf16[1024,128]{1,0:T(8,128)(2,1)}, u32[]{:S(2)}, u32[]{:S(2)}) collective-permute-start(bf16[1024,128]{1,0:T(8,128)(2,1)} %get-tuple-element.50), channel_id=1, source_target_pairs={{0,48},{8,56},{16,0},{24,8},{32,16},{40,24},{48,32},{56,40},{64,11... | collective-permute-start | bytes 786440 | tf_op jit(solution)/shard_map/ppermute | solution.py:320
  150.0 0.9 collective-permute-start.20
  150.9 2.1 %collective-permute-start.14 = (f32[512,128]{1,0:T(8,128)}, f32[512,128]{1,0:T(8,128)S(1)}, u32[]{:S(2)}, u32[]{:S(2)}) collective-permute-start(f32[512,128]{1,0:T(8,128)} %get-tuple-element.38), channel_id=1, source_target_pairs={{0,8},{8,0},{16,24},{24,16},{32,40},{40,32},{48,56},{56,48},{64,72... | collective-permute-start | bytes 786440 | tf_op jit(solution)/shard_map/ppermute | solution.py:320
  153.0 1.2 add_bitcast_fusion
  154.2 1.4 collective-permute-start.26
  155.6 5.6 %collective-permute-done.18 = bf16[1024,128]{1,0:T(8,128)(2,1)} collective-permute-done((bf16[1024,128]{1,0:T(8,128)(2,1)}, bf16[1024,128]{1,0:T(8,128)(2,1)}, u32[]{:S(2)}, u32[]{:S(2)}) %collective-permute-start.18) | collective-permute-done | bytes 262176 | tf_op jit(solution)/shard_map/ppermute | solution.py:320
  161.2 4.4 %collective-permute-done.20 = bf16[1024,128]{1,0:T(8,128)(2,1)} collective-permute-done((bf16[1024,128]{1,0:T(8,128)(2,1)}, bf16[1024,128]{1,0:T(8,128)(2,1)}, u32[]{:S(2)}, u32[]{:S(2)}) %collective-permute-start.20) | collective-permute-done | bytes 262176 | tf_op jit(solution)/shard_map/ppermute | solution.py:320
  165.6 1.5 fusion.6
  167.1 1.3 collective-permute-start.21
  168.4 0.8 maximum_select_fusion
  169.9 6.4 %collective-permute-done.21 = bf16[1024,128]{1,0:T(8,128)(2,1)S(1)} collective-permute-done((bf16[1024,128]{1,0:T(8,128)(2,1)S(1)}, bf16[1024,128]{1,0:T(8,128)(2,1)S(1)}, u32[]{:S(2)}, u32[]{:S(2)}) %collective-permute-start.21) | collective-permute-done | bytes 262176 | tf_op jit(solution)/shard_map/ppermute | solution.py:320
  176.4 0.8 slice_add_fusion
  (104 shorter events, 8.9 us)
Async XLA Ops:
  7.2 8.8 %copy-start.18 = (s32[5]{0:T(128)S(1)}, s32[5]{0:T(128)}, u32[]{:S(2)}) copy-start(s32[5]{0:T(128)} %constant.89) | copy-start | bytes 64
  7.2 8.8 %copy-start.17 = (s32[3]{0:T(128)S(1)}, s32[3]{0:T(128)}, u32[]{:S(2)}) copy-start(s32[3]{0:T(128)} %constant.87) | copy-start | bytes 40
  7.2 7.6 %copy-start.9 = (bf16[512,128]{1,0:T(8,128)(2,1)S(1)}, bf16[512,128]{1,0:T(8,128)(2,1)}, u32[]{:S(2)}) copy-start(bf16[512,128]{1,0:T(8,128)(2,1)} %param.15) | copy-start | bytes 393220
  7.2 7.6 %copy-start.8 = (bf16[512,128]{1,0:T(8,128)(2,1)S(1)}, bf16[512,128]{1,0:T(8,128)(2,1)}, u32[]{:S(2)}) copy-start(bf16[512,128]{1,0:T(8,128)(2,1)} %param.16) | copy-start | bytes 393220
  7.2 66.6 %all-gather.2.cloned.1.call-start = ((), (), s32[]{:S(2)}) async-start(), calls=%async_computation.2 | async-start | bytes 4718592 | tf_op jit(solution)/shard_map/all_gather | solution.py:352
  7.9 12.3 %copy-start.16 = (s32[4]{0:T(128)S(1)}, s32[4]{0:T(128)}, u32[]{:S(2)}) copy-start(s32[4]{0:T(128)} %constant.85) | copy-start | bytes 52
  8.0 169.2 %reduce-scatter.2.cloned.1.call-start = ((), (), s32[]{:S(2)}) async-start(), calls=%async_computation.1 | async-start | bytes 4718592 | tf_op jit(solution)/shard_map/reduce_scatter | solution.py:396
  9.8 16.8 %copy-start.6 = (bf16[1024,128]{1,0:T(8,128)(2,1)}, bf16[1024,128]{1,0:T(8,128)(2,1)S(1)}, u32[]{:S(2)}) copy-start(bf16[1024,128]{1,0:T(8,128)(2,1)S(1)} %constant_dynamic-update-slice_fusion.refs_2_.refs_7_) | copy-start | bytes 786436
  9.9 8.9 %collective-permute-start.1 = (bf16[1024,128]{1,0:T(8,128)(2,1)S(1)}, bf16[1024,128]{1,0:T(8,128)(2,1)S(1)}, u32[]{:S(2)}, u32[]{:S(2)}) collective-permute-start(bf16[1024,128]{1,0:T(8,128)(2,1)S(1)} %constant_dynamic-update-slice_fusion.refs_2_.refs_7_), channel_id=1, source_target_pairs={{0,64},{8,72},{16,80},{24,88},{32,96},{40,104},{48,112},{56,120},{... | collective-permute-start | bytes 786440 | tf_op jit(solution)/shard_map/ppermute | solution.py:320
  14.8 22.7 %copy-start.15 = (s32[32,12]{0,1:T(8,128)S(1)}, s32[32,12]{0,1:T(8,128)}, u32[]{:S(2)}) copy-start(s32[32,12]{0,1:T(8,128)} %param.18) | copy-start | bytes 4612
  14.9 29.9 %collective-permute-start = (bf16[1536,128]{1,0:T(8,128)(2,1)S(1)}, bf16[1536,128]{1,0:T(8,128)(2,1)S(1)}, u32[]{:S(2)}, u32[]{:S(2)}) collective-permute-start(bf16[1536,128]{1,0:T(8,128)(2,1)S(1)} %pad_maximum_fusion), channel_id=1, source_target_pairs={{0,8},{8,0},{16,24},{24,16},{32,40},{40,32},{48,56},{56,48},{64,72... | collective-permute-start | bytes 1179656 | tf_op jit(solution)/shard_map/ppermute | solution.py:320
  18.8 37.2 %copy-start.11 = (bf16[1024,128]{1,0:T(8,128)(2,1)}, bf16[1024,128]{1,0:T(8,128)(2,1)S(1)}, u32[]{:S(2)}) copy-start(bf16[1024,128]{1,0:T(8,128)(2,1)S(1)} %collective-permute-done.1.refs_5_.refs_10_) | copy-start | bytes 786436
  18.8 7.7 %collective-permute-start.2 = (bf16[1024,128]{1,0:T(8,128)(2,1)S(1)}, bf16[1024,128]{1,0:T(8,128)(2,1)S(1)}, u32[]{:S(2)}, u32[]{:S(2)}) collective-permute-start(bf16[1024,128]{1,0:T(8,128)(2,1)S(1)} %get-tuple-element.58), channel_id=1, source_target_pairs={{0,16},{8,24},{16,32},{24,40},{32,48},{40,56},{48,0},{56,8},{64,80... | collective-permute-start | bytes 786440 | tf_op jit(solution)/shard_map/ppermute | solution.py:320
  20.3 13.0 %collective-permute-start.3 = (bf16[1024,128]{1,0:T(8,128)(2,1)S(1)}, bf16[1024,128]{1,0:T(8,128)(2,1)S(1)}, u32[]{:S(2)}, u32[]{:S(2)}) collective-permute-start(bf16[1024,128]{1,0:T(8,128)(2,1)S(1)} %get-tuple-element.57), channel_id=1, source_target_pairs={{0,32},{8,40},{16,48},{24,56},{32,0},{40,8},{48,16},{56,24},{64,96... | collective-permute-start | bytes 786440 | tf_op jit(solution)/shard_map/ppermute | solution.py:320
  33.4 27.6 %copy-start.13 = (bf16[2048,128]{1,0:T(8,128)(2,1)}, bf16[2048,128]{1,0:T(8,128)(2,1)S(1)}, u32[]{:S(2)}) copy-start(bf16[2048,128]{1,0:T(8,128)(2,1)S(1)} %constant_dynamic-update-slice_fusion.2.refs_4_.refs_9_) | copy-start | bytes 1572868
  33.4 13.4 %collective-permute-start.8 = (bf16[2048,128]{1,0:T(8,128)(2,1)S(1)}, bf16[2048,128]{1,0:T(8,128)(2,1)S(1)}, u32[]{:S(2)}, u32[]{:S(2)}) collective-permute-start(bf16[2048,128]{1,0:T(8,128)(2,1)S(1)} %constant_dynamic-update-slice_fusion.2.refs_4_.refs_9_), channel_id=1, source_target_pairs={{0,64},{8,72},{16,80},{24,88},{32,96},{40,104},{48,112},{56,120},{... | collective-permute-start | bytes 1572872 | tf_op jit(solution)/shard_map/ppermute | solution.py:320
  37.8 7.0 %collective-permute-start.4 = (bf16[1024,128]{1,0:T(8,128)(2,1)S(1)}, bf16[1024,128]{1,0:T(8,128)(2,1)S(1)}, u32[]{:S(2)}, u32[]{:S(2)}) collective-permute-start(bf16[1024,128]{1,0:T(8,128)(2,1)S(1)} %get-tuple-element.56), channel_id=1, source_target_pairs={{0,48},{8,56},{16,0},{24,8},{32,16},{40,24},{48,32},{56,40},{64,11... | collective-permute-start | bytes 786440 | tf_op jit(solution)/shard_map/ppermute | solution.py:320
  37.9 14.6 %collective-permute-start.9 = (bf16[1024,128]{1,0:T(8,128)(2,1)S(1)}, bf16[1024,128]{1,0:T(8,128)(2,1)S(1)}, u32[]{:S(2)}, u32[]{:S(2)}) collective-permute-start(bf16[1024,128]{1,0:T(8,128)(2,1)S(1)} %collective-permute-done.1.refs_5_.refs_10_), channel_id=1, source_target_pairs={{0,64},{8,72},{16,80},{24,88},{32,96},{40,104},{48,112},{56,120},{... | collective-permute-start | bytes 786440 | tf_op jit(solution)/shard_map/ppermute | solution.py:320
  41.0 19.9 %collective-permute-start.5 = (bf16[2048,128]{1,0:T(8,128)(2,1)S(1)}, bf16[2048,128]{1,0:T(8,128)(2,1)}, u32[]{:S(2)}, u32[]{:S(2)}) collective-permute-start(bf16[2048,128]{1,0:T(8,128)(2,1)S(1)} %constant_dynamic-update-slice_fusion.2.refs_4_.refs_9_), channel_id=1, source_target_pairs={{0,8},{8,0},{16,24},{24,16},{32,40},{40,32},{48,56},{56,48},{64,72... | collective-permute-start | bytes 1572872 | tf_op jit(solution)/shard_map/ppermute | solution.py:320
  44.8 11.2 %copy-start.14 = (bf16[1536,128]{1,0:T(8,128)(2,1)}, bf16[1536,128]{1,0:T(8,128)(2,1)S(1)}, u32[]{:S(2)}) copy-start(bf16[1536,128]{1,0:T(8,128)(2,1)S(1)} %collective-permute-done.refs_3_.refs_8_) | copy-start | bytes 1179652
  44.8 16.1 %collective-permute-start.6 = (bf16[1024,128]{1,0:T(8,128)(2,1)S(1)}, bf16[1024,128]{1,0:T(8,128)(2,1)S(1)}, u32[]{:S(2)}, u32[]{:S(2)}) collective-permute-start(bf16[1024,128]{1,0:T(8,128)(2,1)S(1)} %collective-permute-done.1.refs_5_.refs_10_), channel_id=1, source_target_pairs={{0,8},{8,0},{16,24},{24,16},{32,40},{40,32},{48,56},{56,48},{64,72... | collective-permute-start | bytes 786440 | tf_op jit(solution)/shard_map/ppermute | solution.py:320
  44.8 16.1 %copy-start.21 = (bf16[1024,128]{1,0:T(8,128)(2,1)}, bf16[1024,128]{1,0:T(8,128)(2,1)S(1)}, u32[]{:S(2)}) copy-start(bf16[1024,128]{1,0:T(8,128)(2,1)S(1)} %collective-permute-done.4.refs_6_.refs_11_) | copy-start | bytes 786436
  44.8 16.1 %collective-permute-start.7 = (bf16[1024,128]{1,0:T(8,128)(2,1)S(1)}, bf16[1024,128]{1,0:T(8,128)(2,1)S(1)}, u32[]{:S(2)}, u32[]{:S(2)}) collective-permute-start(bf16[1024,128]{1,0:T(8,128)(2,1)S(1)} %collective-permute-done.4.refs_6_.refs_11_), channel_id=1, source_target_pairs={{0,8},{8,0},{16,24},{24,16},{32,40},{40,32},{48,56},{56,48},{64,72... | collective-permute-start | bytes 786440 | tf_op jit(solution)/shard_map/ppermute | solution.py:320
  46.8 17.1 %copy-start.19 = (bf16[2048,128]{1,0:T(8,128)(2,1)}, bf16[2048,128]{1,0:T(8,128)(2,1)S(1)}, u32[]{:S(2)}) copy-start(bf16[2048,128]{1,0:T(8,128)(2,1)S(1)} %collective-permute-done.8.refs_4_.refs_7_) | copy-start | bytes 1572868
  46.8 17.2 %collective-permute-start.10 = (bf16[2048,128]{1,0:T(8,128)(2,1)S(1)}, bf16[2048,128]{1,0:T(8,128)(2,1)S(1)}, u32[]{:S(2)}, u32[]{:S(2)}) collective-permute-start(bf16[2048,128]{1,0:T(8,128)(2,1)S(1)} %collective-permute-done.8.refs_4_.refs_7_), channel_id=1, source_target_pairs={{0,8},{8,0},{16,24},{24,16},{32,40},{40,32},{48,56},{56,48},{64,72... | collective-permute-start | bytes 1572872 | tf_op jit(solution)/shard_map/ppermute | solution.py:320
  52.5 11.5 %copy-start.23 = (bf16[1024,128]{1,0:T(8,128)(2,1)}, bf16[1024,128]{1,0:T(8,128)(2,1)S(1)}, u32[]{:S(2)}) copy-start(bf16[1024,128]{1,0:T(8,128)(2,1)S(1)} %collective-permute-done.9.refs_5_.refs_8_) | copy-start | bytes 786436
  52.5 11.5 %collective-permute-start.11 = (bf16[1024,128]{1,0:T(8,128)(2,1)S(1)}, bf16[1024,128]{1,0:T(8,128)(2,1)}, u32[]{:S(2)}, u32[]{:S(2)}) collective-permute-start(bf16[1024,128]{1,0:T(8,128)(2,1)S(1)} %collective-permute-done.9.refs_5_.refs_8_), channel_id=1, source_target_pairs={{0,8},{8,0},{16,24},{24,16},{32,40},{40,32},{48,56},{56,48},{64,72... | collective-permute-start | bytes 786440 | tf_op jit(solution)/shard_map/ppermute | solution.py:320
  64.8 5.0 %copy-start = (bf16[256,4096]{1,0:T(8,128)(2,1)S(1)}, bf16[256,4096]{1,0:T(8,128)(2,1)}, u32[]{:S(2)}) copy-start(bf16[256,4096]{1,0:T(8,128)(2,1)} %refs_7_.1) | copy-start | bytes 6291460
  67.1 1.6 collective-permute-start.12
  69.8 3.3 %copy-start.1 = (bf16[512,256]{1,0:T(8,128)(2,1)}, bf16[512,256]{1,0:T(8,128)(2,1)S(1)}, u32[]{:S(2)}) copy-start(bf16[512,256]{1,0:T(8,128)(2,1)S(1)} %maximum_select_fusion.1.a_ref) | copy-start | bytes 786436
  81.3 1.6 collective-permute-start.13
  81.6 14.0 %collective-permute-start.22 = (bf16[16,256,128]{2,1,0:T(8,128)(2,1)}, bf16[16,256,128]{2,1,0:T(8,128)(2,1)S(1)}, u32[]{:S(2)}, u32[]{:S(2)}) collective-permute-start(bf16[16,256,128]{2,1,0:T(8,128)(2,1)} %get-tuple-element.44), channel_id=1, source_target_pairs={{0,8},{8,0},{16,24},{24,16},{32,40},{40,32},{48,56},{56,48},{64,72... | collective-permute-start | bytes 3145736 | tf_op jit(solution)/shard_map/ppermute | solution.py:320
  87.2 9.8 %collective-permute-start.16 = (bf16[3072,128]{1,0:T(8,128)(2,1)}, bf16[3072,128]{1,0:T(8,128)(2,1)}, u32[]{:S(2)}, u32[]{:S(2)}) collective-permute-start(bf16[3072,128]{1,0:T(8,128)(2,1)} %get-tuple-element.42), channel_id=1, source_target_pairs={{0,8},{8,0},{16,24},{24,16},{32,40},{40,32},{48,56},{56,48},{64,72... | collective-permute-start | bytes 2359304 | tf_op jit(solution)/shard_map/ppermute | solution.py:320
  87.4 8.2 %copy-start.3 = (bf16[16,256,128]{2,1,0:T(8,128)(2,1)S(1)}, bf16[16,256,128]{2,1,0:T(8,128)(2,1)}, u32[]{:S(2)}) copy-start(bf16[16,256,128]{2,1,0:T(8,128)(2,1)} %get-tuple-element.43) | copy-start | bytes 3145732
  95.2 43.1 %collective-permute-start.15 = (bf16[5120,128]{1,0:T(8,128)(2,1)}, bf16[5120,128]{1,0:T(8,128)(2,1)S(1)}, u32[]{:S(2)}, u32[]{:S(2)}) collective-permute-start(bf16[5120,128]{1,0:T(8,128)(2,1)} %get-tuple-element.40), channel_id=1, source_target_pairs={{0,8},{8,0},{16,24},{24,16},{32,40},{40,32},{48,56},{56,48},{64,72... | collective-permute-start | bytes 3932168 | tf_op jit(solution)/shard_map/ppermute | solution.py:320
  95.8 13.5 %collective-permute-start.23 = (bf16[8,256,128]{2,1,0:T(8,128)(2,1)S(1)}, bf16[8,256,128]{2,1,0:T(8,128)(2,1)S(1)}, u32[]{:S(2)}, u32[]{:S(2)}) collective-permute-start(bf16[8,256,128]{2,1,0:T(8,128)(2,1)S(1)} %add_convert_fusion.1), channel_id=1, source_target_pairs={{0,16},{8,24},{16,0},{24,8},{32,48},{40,56},{48,32},{56,40},{64,80... | collective-permute-start | bytes 1572872 | tf_op jit(solution)/shard_map/ppermute | solution.py:320
  97.0 41.3 %copy-start.2 = (bf16[5120,128]{1,0:T(8,128)(2,1)S(1)}, bf16[5120,128]{1,0:T(8,128)(2,1)}, u32[]{:S(2)}) copy-start(bf16[5120,128]{1,0:T(8,128)(2,1)} %get-tuple-element.39) | copy-start | bytes 3932164
  98.4 39.8 %collective-permute-start.17 = (bf16[3072,128]{1,0:T(8,128)(2,1)S(1)}, bf16[3072,128]{1,0:T(8,128)(2,1)S(1)}, u32[]{:S(2)}, u32[]{:S(2)}) collective-permute-start(bf16[3072,128]{1,0:T(8,128)(2,1)S(1)} %add_convert_fusion), channel_id=1, source_target_pairs={{64,0},{72,8},{80,16},{88,24},{96,32},{104,40},{112,48},{120,56},{... | collective-permute-start | bytes 2359304 | tf_op jit(solution)/shard_map/ppermute | solution.py:320
  109.3 30.1 %copy-start.7 = (bf16[8,256,128]{2,1,0:T(8,128)(2,1)}, bf16[8,256,128]{2,1,0:T(8,128)(2,1)S(1)}, u32[]{:S(2)}) copy-start(bf16[8,256,128]{2,1,0:T(8,128)(2,1)S(1)} %collective-permute-done.23) | copy-start | bytes 1572868
  110.6 24.7 %collective-permute-start.24 = (bf16[4,256,128]{2,1,0:T(8,128)(2,1)S(1)}, bf16[4,256,128]{2,1,0:T(8,128)(2,1)S(1)}, u32[]{:S(2)}, u32[]{:S(2)}) collective-permute-start(bf16[4,256,128]{2,1,0:T(8,128)(2,1)S(1)} %add_convert_fusion.2), channel_id=1, source_target_pairs={{0,64},{8,72},{16,80},{24,88},{32,96},{40,104},{48,112},{56,120},{... | collective-permute-start | bytes 786440 | tf_op jit(solution)/shard_map/ppermute | solution.py:320
  136.5 16.5 %collective-permute-start.25 = (bf16[2,256,128]{2,1,0:T(8,128)(2,1)S(1)}, bf16[2,256,128]{2,1,0:T(8,128)(2,1)}, u32[]{:S(2)}, u32[]{:S(2)}) collective-permute-start(bf16[2,256,128]{2,1,0:T(8,128)(2,1)S(1)} %add_convert_fusion.6), channel_id=1, source_target_pairs={{0,128},{8,136},{16,144},{24,152},{32,160},{40,168},{48,176},{56,1... | collective-permute-start | bytes 393224 | tf_op jit(solution)/shard_map/ppermute | solution.py:320
  139.3 21.8 %collective-permute-start.18 = (bf16[1024,128]{1,0:T(8,128)(2,1)}, bf16[1024,128]{1,0:T(8,128)(2,1)}, u32[]{:S(2)}, u32[]{:S(2)}) collective-permute-start(bf16[1024,128]{1,0:T(8,128)(2,1)} %get-tuple-element.50), channel_id=1, source_target_pairs={{0,48},{8,56},{16,0},{24,8},{32,16},{40,24},{48,32},{56,40},{64,11... | collective-permute-start | bytes 786440 | tf_op jit(solution)/shard_map/ppermute | solution.py:320
  149.2 12.0 %collective-permute-start.19 = (bf16[1024,128]{1,0:T(8,128)(2,1)}, bf16[1024,128]{1,0:T(8,128)(2,1)}, u32[]{:S(2)}, u32[]{:S(2)}) collective-permute-start(bf16[1024,128]{1,0:T(8,128)(2,1)} %get-tuple-element.49), channel_id=1, source_target_pairs={{0,32},{8,40},{16,48},{24,56},{32,0},{40,8},{48,16},{56,24},{64,96... | collective-permute-start | bytes 786440 | tf_op jit(solution)/shard_map/ppermute | solution.py:320
  150.0 15.6 %collective-permute-start.20 = (bf16[1024,128]{1,0:T(8,128)(2,1)}, bf16[1024,128]{1,0:T(8,128)(2,1)}, u32[]{:S(2)}, u32[]{:S(2)}) collective-permute-start(bf16[1024,128]{1,0:T(8,128)(2,1)} %get-tuple-element.53), channel_id=1, source_target_pairs={{0,16},{8,24},{16,32},{24,40},{32,48},{40,56},{48,0},{56,8},{64,80... | collective-permute-start | bytes 786440 | tf_op jit(solution)/shard_map/ppermute | solution.py:320
  150.9 17.5 %collective-permute-start.14 = (f32[512,128]{1,0:T(8,128)}, f32[512,128]{1,0:T(8,128)S(1)}, u32[]{:S(2)}, u32[]{:S(2)}) collective-permute-start(f32[512,128]{1,0:T(8,128)} %get-tuple-element.38), channel_id=1, source_target_pairs={{0,8},{8,0},{16,24},{24,16},{32,40},{40,32},{48,56},{56,48},{64,72... | collective-permute-start | bytes 786440 | tf_op jit(solution)/shard_map/ppermute | solution.py:320
  154.2 14.2 %copy-start.12 = (f32[512,128]{1,0:T(8,128)S(1)}, f32[512,128]{1,0:T(8,128)}, u32[]{:S(2)}) copy-start(f32[512,128]{1,0:T(8,128)} %get-tuple-element.37) | copy-start | bytes 786436
  154.2 15.0 %collective-permute-start.26 = (bf16[1,256,128]{2,1,0:T(8,128)(2,1)S(1)}, bf16[1,256,128]{2,1,0:T(8,128)(2,1)S(1)}, u32[]{:S(2)}, u32[]{:S(2)}) collective-permute-start(bf16[1,256,128]{2,1,0:T(8,128)(2,1)S(1)} %get-tuple-element.46), channel_id=1, source_target_pairs={{0,32},{8,40},{16,48},{24,56},{32,0},{40,8},{48,16},{56,24},{64,96... | collective-permute-start | bytes 196616 | tf_op jit(solution)/shard_map/ppermute | solution.py:320
  167.1 9.3 %collective-permute-start.21 = (bf16[1024,128]{1,0:T(8,128)(2,1)S(1)}, bf16[1024,128]{1,0:T(8,128)(2,1)S(1)}, u32[]{:S(2)}, u32[]{:S(2)}) collective-permute-start(bf16[1024,128]{1,0:T(8,128)(2,1)S(1)} %get-tuple-element.47), channel_id=1, source_target_pairs={{64,0},{72,8},{80,16},{88,24},{96,32},{104,40},{112,48},{120,56},{... | collective-permute-start | bytes 786440 | tf_op jit(solution)/shard_map/ppermute | solution.py:320
  (7 other events, 9.1 us)
Sparse Core Ops, SparseCore 0:
  9.8 58.3 all-gather.1
  73.2 65.7 reduce-scatter.1
